TPU v7x, 512 devices: a whole 4x4x16 slice. The times are simulated.
512 devices in a mesh: wide: 64 (over z, y), grp: 8 (over x, core).
Axes of the slice: x: 4, y: 4, z: 16, core: 2. Of those that a mesh axis runs over, the one named last changes fastest.
Arguments:
- amplitudes: bfloat16 [512, 131072], P(('wide', 'grp')), may hold values from -6 to 6
- amplitude_live: int32 [512, 1024], replicated, may hold values from 0 to 1, as said below
- integrals: bfloat16 [2048, 131072], P('grp', 'wide'), may hold values from -0.0234375 to 0.0234375
- integral_live: int32 [16, 1024], P('grp', 'wide'), may hold values 0 or 1
Outputs:
- ladder: bfloat16 [512, 2048], P(('wide', 'grp'))
Inputs may be any that keep to these rules, and one draw needn't show every extreme that they name: `amplitude_live`: entries are 0 or 1. In every row b, among the 16 cd tiles c with c // 16 equal to one index of wide, at most 12 are 1; in every row exactly 12 for at least one such index.
All inputs are finite; a program needn't handle non-finite values. No bound on the sum of `integral_live` on one device may be relied on, other than what follows from the above.
Results may differ from a plain program's by a relative error of at most 0.0018.
Values may be sent and summed in bfloat16 or wider, within the bound.
No kernel may reach another device: no remote copies, remote signals or barrier semaphores. Data moves between devices by JAX's collectives and lax.ppermute only.
A program may use at most 64 MiB of HBM per device.

v0:
```python
import jax
import jax.numpy as jnp
from jax import lax
from jax.sharding import PartitionSpec as P

TW = 128


def per_device(amplitudes, amplitude_live, integrals, integral_live):
    wide_count = lax.axis_size("wide")
    group_count = lax.axis_size("grp")
    wide_index = lax.axis_index("wide")
    group_index = lax.axis_index("grp")
    row_count = amplitudes.shape[0]
    column_tiles = integrals.shape[1] // TW
    ab_tiles = integrals.shape[0] // TW
    own_live = lax.dynamic_index_in_dim(
        amplitude_live, wide_index * group_count + group_index, 0, keepdims=False
    )
    own_live = own_live.reshape(wide_count, column_tiles)
    amp_view = amplitudes.reshape(row_count, wide_count, column_tiles, TW)
    masked = amp_view * own_live.astype(amplitudes.dtype)[None, :, :, None]
    arrived = lax.all_to_all(
        masked.reshape(row_count, wide_count * column_tiles * TW),
        "wide",
        split_axis=1,
        concat_axis=0,
        tiled=True,
    )
    columns = arrived.reshape(wide_count, row_count, column_tiles * TW)
    int_mask = integral_live.astype(integrals.dtype)
    int_used = (
        integrals.reshape(ab_tiles, TW, column_tiles, TW) * int_mask[:, None, :, None]
    ).reshape(ab_tiles * TW, column_tiles * TW)
    partial_sums = lax.dot_general(
        lax.all_gather(columns, "grp", axis=1, tiled=True),
        int_used,
        (((2,), (1,)), ((), ())),
        preferred_element_type=jnp.float32,
    )
    summed = lax.psum_scatter(partial_sums, "wide", scatter_dimension=0, tiled=True)
    finished = summed.reshape(group_count * row_count, ab_tiles * TW).astype(jnp.bfloat16)
    return lax.all_to_all(finished, "grp", split_axis=0, concat_axis=1, tiled=True)


def solution(mesh):
    in_specs = (P(("wide", "grp"), None), P(), P("grp", "wide"), P("grp", "wide"))
    out_specs = P(("wide", "grp"), None)
    return jax.shard_map(
        per_device, mesh=mesh, in_specs=in_specs, out_specs=out_specs, check_vma=False
    )
```

profile of v0, /device:TPU:1, one launch (start us, length us, event | category | flops | bytes accessed | tf_op | source)
XLA Modules:
  0.0 810.6 jit_solution(14417329765814925144)
XLA Ops:
  6.5 0.0 all-gather.3.cloned.1.call-start
  6.5 0.8 convert_reduce_fusion
  7.3 0.1 convert_element_type.27
  7.4 0.2 mul.28
  7.6 0.1 mul.29
  7.7 0.0 copy-start.1
  7.7 1.9 mul.30
  9.6 0.5 broadcast.9
  10.1 2.2 reduce.3
  12.3 0.2 reshape.55
  12.5 38.3 %all_to_all.26 = bf16[64,2,1024]{2,1,0:T(2,128)(2,1)S(1)} all-to-all(bf16[64,2,1024]{2,1,0:T(2,128)(2,1)S(1)} %reshape.55), channel_id=1, replica_groups=mesh['wide'=64,'grp'=8] {'wide'}, dimensions={0} | all-to-all | bytes 524288 | tf_op jit(solution)/shard_map/all_to_all | solution.py:23
  50.7 0.9 reshape.56
  51.6 0.0 all-gather.3.cloned.1.call-update
  51.7 0.0 reduce-scatter.2.cloned.1.call-start
  51.7 0.0 copy-done.1
  51.7 34.5 %all-gather.3.cloned.1.call-done = bf16[1,64,16384]{2,0,1:T(2,128)(2,1)} async-done(((bf16[1,64,2048]{2,0,1:T(2,128)(2,1)}), bf16[1,64,16384]{2,0,1:T(2,128)(2,1)}) %all-gather.3.cloned.1.call-update) | async-done | bytes 2097168 | tf_op jit(solution)/shard_map/all_gather | solution.py:36
  86.2 12.5 %reduce.1 = bf16[64,16384]{1,0:T(8,128)(2,1)S(1)} reduce(bf16[1,64,16384]{2,0,1:T(2,128)(2,1)} %all-gather.3.cloned.1.call-done, bf16[]{:T(256)} %constant.19), dimensions={0}, to_apply=%all-gather.reduce_sub_computation | reduce | bytes 4194306 | tf_op jit(solution)/shard_map/all_gather | solution.py:36
  98.8 0.0 copy-start
  98.8 1.2 copy.7
  100.0 0.2 mul.31
  100.2 0.0 copy-done
  100.2 1.5 fusion.1
  101.7 0.0 reduce-scatter.2.cloned.1.call-update
  101.7 679.5 %reduce-scatter.2.cloned.1.call-done = f32[1,8,256]{2,1,0:T(8,128)} async-done(((f32[64,8,256]{2,1,0:T(8,128)}), f32[1,8,256]{2,1,0:T(8,128)}) %reduce-scatter.2.cloned.1.call-update) | async-done | bytes 8208 | tf_op jit(solution)/shard_map/reduce_scatter | solution.py:41
  781.3 0.7 convert_bitcast_fusion
  782.0 0.6 reduce.4
  782.6 20.5 %all_to_all.27 = bf16[8,2,128]{2,1,0:T(2,128)(2,1)S(1)} all-to-all(bf16[8,2,128]{2,1,0:T(2,128)(2,1)S(1)} %reshape.57), channel_id=1, replica_groups=mesh['wide'=64,'grp'=8] {'grp'}, dimensions={0} | all-to-all | bytes 8192 | tf_op jit(solution)/shard_map/all_to_all | solution.py:43
  803.2 0.6 reshape.58
  (2 shorter events, 0.0 us)
Async XLA Ops:
  6.5 79.7 %all-gather.3.cloned.1.call-start = ((), (), s32[]{:S(2)}) async-start(), calls=%async_computation.4 | async-start | bytes 4718592 | tf_op jit(solution)/shard_map/all_gather | solution.py:36
  7.7 44.0 %copy-start.1 = (s32[2,16]{1,0:T(2,128)S(1)}, s32[2,16]{1,0:T(2,128)}, u32[]{:S(2)}) copy-start(s32[2,16]{1,0:T(2,128)} %param.7) | copy-start | bytes 388
  51.7 729.6 %reduce-scatter.2.cloned.1.call-start = ((), (), s32[]{:S(2)}) async-start(), calls=%async_computation.3 | async-start | bytes 532480 | tf_op jit(solution)/shard_map/reduce_scatter | solution.py:41
  98.8 1.4 copy-start
Sparse Core Ops, SparseCore 0:
  51.8 34.3 all-gather.2
  101.9 679.3 reduce-scatter.1
where the time goes:
time: 811 us
  waiting for transfers between devices  714 us (88%)
  blocking collectives  58.8 us (7%)
  other arithmetic  18.7 us (2%)
  between operations  13.5 us (2%)
    reduce_scatter x1, waiting for transfers between devices, per_device(): lax.psum_scatter(partial_sums, 'wide', scatter_dimension=0, tiled=True)  680 us
    all_to_all x1, blocking collectives, per_device(): lax.all_to_all(masked.reshape(row_count, wide_count * column_tiles * TW),...  38.3 us
    all_gather x1, waiting for transfers between devices, per_device(): lax.all_gather(columns, 'grp', axis=1, tiled=True)  34.5 us
    all_to_all x1, blocking collectives, per_device(): lax.all_to_all(finished, 'grp', split_axis=0, concat_axis=1, tiled=True)  20.5 us
  transfers between devices with their start and end apart: 2, of which 2 were waited for; matrix products, arithmetic and copies ran while one was open for 0% of the time, Pallas kernels for 0%

commit v1 on v0

v1 whole, which is shorter than its diff:
```python
import functools

import jax
import jax.numpy as jnp
from jax import lax
from jax.experimental import pallas as pl
from jax.experimental.pallas import tpu as pltpu
from jax.sharding import Mesh, PartitionSpec as P

TW = 128
NZ, NY, NX, NC = 16, 4, 4, 2
NW = NZ * NY
CT = 16
CAP = 12
DROP = CT - CAP
F32 = jnp.float32
BF16 = jnp.bfloat16


def iota(shape, dim):
    return lax.broadcasted_iota(jnp.int32, shape, dim)


def dot(a, b):
    return lax.dot_general(a, b, (((1,), (0,)), ((), ())), preferred_element_type=F32)


def before_matrix():
    rows, cols = iota((TW, TW), 0), iota((TW, TW), 1)
    same = (rows // CT) == (cols // CT)
    return jnp.where(same & (rows < cols), 1.0, 0.0).astype(BF16)


def pack_kernel(me_ref, live_ref, amp_ref, out_ref):
    sub = me_ref[0] % 8
    live = live_ref[...].astype(F32)
    row = jnp.sum(jnp.where(iota(live.shape, 0) == sub, live, 0.0), axis=0, keepdims=True)
    dead = jnp.broadcast_to(1.0 - row, (8, NW * CT)).astype(BF16)
    before = before_matrix()
    lanes = 2 * TW
    out_row, col = iota((lanes, lanes), 0), iota((lanes, lanes), 1)
    slot = jnp.where(out_row // CT == col // CT, out_row % CT, -7).astype(F32)
    tile = (iota((1, lanes), 1) % CT).astype(F32)
    for q in range(4):
        dead_q = dead[:, q * lanes : (q + 1) * lanes]
        count = jnp.concatenate([dot(dead_q[:, :TW], before), dot(dead_q[:, TW:], before)], axis=1)[0:1]
        is_dead = dead_q[0:1].astype(F32)
        dropped = (is_dead > 0.5) & (count < DROP - 0.5)
        key = jnp.where(dropped, -1.0, tile - jnp.minimum(count, float(DROP)))
        pick = jnp.where(slot == key, 1.0, 0.0).astype(BF16)
        packed = dot(pick, amp_ref[q * lanes : (q + 1) * lanes, :]).astype(BF16)
        for i in range(16):
            z, y = q * 4 + i // NY, i % NY
            out_ref[y * NZ + z] = packed[i * CT : i * CT + CAP, :]


def pack(me, live, amp_tiles):
    return pl.pallas_call(
        pack_kernel,
        out_shape=jax.ShapeDtypeStruct((NW, CAP, TW), BF16),
        grid_spec=pltpu.PrefetchScalarGridSpec(
            num_scalar_prefetch=1,
            grid=(1,),
            in_specs=[
                pl.BlockSpec((8, NW * CT), lambda i, me: (me[0] // 8, 0)),
                pl.BlockSpec((NW * CT, TW), lambda i, me: (0, 0)),
            ],
            out_specs=pl.BlockSpec((NW, CAP, TW), lambda i, me: (0, 0, 0)),
        ),
        name="pack",
    )(me, live, amp_tiles)


def ladder_kernel(ids_ref, live_ref, amp_ref, own_ref, other_ref, out_ref, used_ref):
    wide, core = ids_ref[0], ids_ref[1]
    rows = NX * NW
    r, g = iota((rows, 512), 0), iota((rows, 512), 1)
    rx, ry, rz = r // NW, (r // NZ) % NY, r % NZ
    source = ((rz * NY + ry) * NX + rx) * NC + core
    pick = jnp.where(g == source, 1.0, 0.0).astype(BF16)
    live = dot(pick, live_ref[...].astype(F32).astype(BF16)).astype(BF16)
    base = (wide % 8) * CT
    lane, c = iota((TW, TW), 0), iota((TW, TW), 1)
    take = jnp.where((lane == base + c) & (c < CT), 1.0, 0.0).astype(BF16)
    prior = jnp.where((lane >= base) & (lane < base + c) & (c < CT), 1.0, 0.0).astype(BF16)
    here = dot(live, take)
    count = dot((1.0 - live.astype(F32)).astype(BF16), prior)
    code = jnp.where(here > 0.5, jnp.minimum(count, float(DROP)), 9.0).astype(BF16)
    spread_row, spread_col = iota((TW, CT * TW), 0), iota((TW, CT * TW), 1)
    spread = jnp.where(spread_row == spread_col // TW, 1.0, 0.0).astype(BF16)
    codes = dot(code, spread).astype(BF16)
    for t in range(CT):
        code_t = codes[:, t * TW : (t + 1) * TW]
        value = jnp.zeros((rows, TW), BF16)
        for d in range(DROP + 1):
            if 0 <= t - d < CAP:
                value = jnp.where(code_t == d, amp_ref[t - d], value)
        used_ref[:, t * TW : (t + 1) * TW] = value
    used = used_ref[...]
    for ref, column in ((own_ref, core), (other_ref, 1 - core)):
        sums = lax.dot_general(used, ref[...], (((1,), (1,)), ((), ())), preferred_element_type=F32)
        for y in range(NY):
            for x in range(NX):
                at = x * NW + y * NZ
                out_ref[y, column, x * NZ : (x + 1) * NZ, :] = sums[at : at + NZ, :]


def ladder(ids, live, amp, own, other):
    whole = lambda *dims: pl.BlockSpec(dims, lambda i, ids: (0,) * len(dims))
    return pl.pallas_call(
        ladder_kernel,
        out_shape=jax.ShapeDtypeStruct((NY, NC, NX * NZ, 256), F32),
        grid_spec=pltpu.PrefetchScalarGridSpec(
            num_scalar_prefetch=1,
            grid=(1,),
            in_specs=[
                pl.BlockSpec((512, TW), lambda i, ids: (0, ids[0] // 8)),
                whole(CAP, NX * NW, TW),
                whole(256, CT * TW),
                whole(256, CT * TW),
            ],
            out_specs=whole(NY, NC, NX * NZ, 256),
            scratch_shapes=[pltpu.VMEM((NX * NW, CT * TW), BF16)],
        ),
        compiler_params=pltpu.CompilerParams(vmem_limit_bytes=40 * 1024 * 1024),
        name="ladder",
    )(ids, live, amp, own, other)


def per_device(amplitudes, amplitude_live, integrals, integral_live):
    wide = lax.axis_index("z") * NY + lax.axis_index("y")
    core = lax.axis_index("c")
    me = (wide * NX + lax.axis_index("x")) * NC + core
    mask = integral_live.astype(BF16)
    own = (integrals.reshape(2, TW, CT, TW) * mask[:, None, :, None]).reshape(2 * TW, CT * TW)
    other = lax.ppermute(own, "c", [(0, 1), (1, 0)])
    packed = pack(me.reshape(1), amplitude_live, amplitudes.reshape(NW * CT, TW))
    arrived = lax.all_to_all(packed, ("y", "z"), 0, 0, tiled=True)
    gathered = lax.all_gather(arrived.transpose(1, 0, 2), "x", axis=1, tiled=True)
    sums = ladder(jnp.stack([wide, core]), amplitude_live, gathered, own, other)
    sums = lax.all_to_all(sums, "y", 0, 0, tiled=True).sum(axis=0)
    sums = lax.all_to_all(sums.transpose(1, 0, 2), ("x", "z"), 0, 0, tiled=True)
    return sums.reshape(NX, NZ, NC * 256).sum(axis=1).reshape(1, NX * NC * 256).astype(BF16)


def solution(mesh):
    fine = Mesh(mesh.devices.reshape(NZ, NY, NX, NC), ("z", "y", "x", "c"))
    wide, grp = ("z", "y"), ("x", "c")
    return jax.shard_map(
        per_device,
        mesh=fine,
        in_specs=(P(wide + grp, None), P(), P(grp, wide), P(grp, wide)),
        out_specs=P(wide + grp, None),
        check_vma=False,
    )
```

time: 811 us -> 96.3 us (0.12)
  the two profiles are of different devices: /device:TPU:1 before, /device:TPU:2 now
where the time goes in v1:
time: 96.3 us; the launch traced here: 96 us
  blocking collectives  46.6 us (48%)
  starting transfers between devices  20.7 us (21%)
  waiting for transfers between devices  17.1 us (18%)
  Pallas kernels  5.49 us (6%)
  other arithmetic  4.94 us (5%)
  local copies, waits for them, and re-layouts  1.08 us (1%)
    all_to_all x1, blocking collectives, per_device(): sums = lax.all_to_all(sums.transpose(1, 0, 2), ('x', 'z'), 0, 0, tiled=True)  21.1 us
    all_to_all x1, starting transfers between devices, per_device(): arrived = lax.all_to_all(packed, ('y', 'z'), 0, 0, tiled=True)  18.7 us
    all_to_all x1, waiting for transfers between devices, per_device(): arrived = lax.all_to_all(packed, ('y', 'z'), 0, 0, tiled=True)  17.1 us
    all_gather x1, blocking collectives, per_device(): lax.all_gather(arrived.transpose(1, 0, 2), 'x', axis=1, tiled=True)  13.4 us
    all_to_all x1, blocking collectives, per_device(): sums = lax.all_to_all(sums, 'y', 0, 0, tiled=True).sum(axis=0)  12.2 us
    pallas_call x1, Pallas kernels, ladder(): pl.pallas_call(ladder_kernel, out_shape=jax.ShapeDtypeStruct((NY, NC, NX...  3.22 us
    unnamed x1, other arithmetic  3.18 us
    pallas_call x1, Pallas kernels, pack(): pl.pallas_call(pack_kernel, out_shape=jax.ShapeDtypeStruct((NW, CAP, TW),...  2.27 us
  transfers between devices with their start and end apart: 2, of which 1 were waited for; matrix products, arithmetic and copies ran while one was open for 2% of the time, Pallas kernels for 0%

profile of v1, /device:TPU:2, one launch (start us, length us, event | category | flops | bytes accessed | tf_op | source)
XLA Modules:
  0.0 96.0 jit_solution(6387447098588687082)
XLA Ops:
  0.0 0.0 copy-start.1
  0.0 3.2 %reduce = bf16[131072]{0:T(1024)(128)(2,1)} reduce(bf16[1,131072]{1,0:T(2,128)(2,1)} %param.4, bf16[]{:T(256)} %constant.25), dimensions={0}, to_apply=%param.4.reduce_sub_computation | reduce | bytes 524290 | tf_op args[0]
  3.2 2.3 %pack.1 = bf16[64,12,128]{2,1,0:T(8,128)(2,1)} custom-call(s32[1]{0:T(128)} %bitcast.2.me_ref, s32[512,1024]{1,0:T(8,128)} %live_ref.3, bf16[1024,128]{1,0:T(8,128)(2,1)} %bitcast.18), custom_call_target="tpu_custom_call" | custom-call | tf_op jit(solution)/shard_map/pack/pallas_call | solution.py:58
  5.5 18.7 %all-to-all-start = ((bf16[64,12,128]{2,1,0:T(8,128)(2,1)}), bf16[64,12,128]{2,1,0:T(8,128)(2,1)S(1)}, u32[]{:S(2)}, u32[]{:S(2)}) async-start(bf16[64,12,128]{2,1,0:T(8,128)(2,1)} %pack.1), calls=%async_computation | async-start | bytes 524288 | tf_op jit(solution)/shard_map/all_to_all | solution.py:138
  24.2 0.0 copy-done.1
  24.2 0.2 mul.23
  24.4 0.0 copy-start
  24.4 1.6 %bitcast_multiply_fusion.own_ref = bf16[256,2048]{1,0:T(8,128)(2,1)S(1)} fusion(bf16[256,2048]{1,0:T(8,128)(2,1)} %param.6, bf16[32,8,16,128]{3,2,1,0:T(8,128)(2,1)S(1)} %bitcast.17), kind=kLoop, calls=%fused_computation | loop fusion | flops 524288 | bytes 3145728 | tf_op jit(solution)/shard_map/mul | solution.py:135
  26.0 1.9 %collective-permute-start = (bf16[256,2048]{1,0:T(8,128)(2,1)S(1)}, bf16[256,2048]{1,0:T(8,128)(2,1)}, u32[]{:S(2)}, u32[]{:S(2)}) collective-permute-start(bf16[256,2048]{1,0:T(8,128)(2,1)S(1)} %bitcast_multiply_fusion.own_ref), channel_id=1, source_target_pairs={{0,1},{1,0},{2,3},{3,2},{4,5},{5,4},{6,7},{7,6},{8,9},{9,8},{10,11... | collective-permute-start | bytes 3145736 | tf_op jit(solution)/shard_map/ppermute | solution.py:136
  28.0 0.1 pad_add_fusion.ids_ref
  28.1 17.1 %all-to-all-done = bf16[64,12,128]{2,1,0:T(8,128)(2,1)S(1)} async-done(((bf16[64,12,128]{2,1,0:T(8,128)(2,1)}), bf16[64,12,128]{2,1,0:T(8,128)(2,1)S(1)}, u32[]{:S(2)}, u32[]{:S(2)}) %all-to-all-start) | async-done | bytes 196640 | tf_op jit(solution)/shard_map/all_to_all | solution.py:138
  45.2 0.1 copy.15
  45.2 13.4 %all_gather.3.amp_ref = bf16[12,256,128]{2,1,0:T(8,128)(2,1)S(1)} all-gather(bf16[12,64,128]{2,1,0:T(8,128)(2,1)S(1)} %bitcast.19), channel_id=1, replica_groups=mesh['z'=16,'y'=4,'x'=4,'c'=2] {'x'}, dimensions={1}, use_global_device_ids=true | all-gather | bytes 983040 | tf_op jit(solution)/shard_map/all_gather | solution.py:139
  58.6 0.0 collective-permute-done.other_ref
  58.6 0.0 copy-done
  58.6 3.2 %ladder.1 = f32[4,2,64,256]{3,2,1,0:T(8,128)S(1)} custom-call(s32[2]{0:T(128)S(1)} %pad_add_fusion.ids_ref, s32[512,1024]{1,0:T(8,128)S(1)} %copy-done, bf16[12,256,128]{2,1,0:T(8,128)(2,1)S(1)} %all_gather.3.amp_ref, bf16[256,2048]{1,0:T(8,128)(2,1)S(1)} %bitcast_multiply_fusion.own_ref, bf16[256,2048]{1,0:T(8,128)(2,1)} %collective-permute-done.other_ref), custom_call_target="tpu_custom_call" | custom-call | tf_op jit(solution)/shard_map/ladder/pallas_call | solution.py:110
  61.8 12.2 %all_to_all.15 = f32[4,2,64,256]{3,2,1,0:T(8,128)S(1)} all-to-all(f32[4,2,64,256]{3,2,1,0:T(8,128)S(1)} %ladder.1), channel_id=1, replica_groups=mesh['z'=16,'y'=4,'x'=4,'c'=2] {'y'}, dimensions={0} | all-to-all | bytes 1048576 | tf_op jit(solution)/shard_map/all_to_all | solution.py:141
  74.0 0.1 copy.10
  74.1 21.1 %all_to_all.16 = f32[64,2,256]{2,1,0:T(2,128)S(1)} all-to-all(f32[64,2,256]{2,1,0:T(2,128)S(1)} %copy.10), channel_id=1, replica_groups=mesh['z'=16,'y'=4,'x'=4,'c'=2] {'x','z'}, dimensions={0} | all-to-all | bytes 262144 | tf_op jit(solution)/shard_map/all_to_all | solution.py:142
  95.2 0.1 reshape.29
  95.3 0.6 copy.12
  (3 shorter events, 0.1 us)
Async XLA Ops:
  0.0 24.2 %copy-start.1 = (s32[2,16]{1,0:T(2,128)S(1)}, s32[2,16]{1,0:T(2,128)}, u32[]{:S(2)}) copy-start(s32[2,16]{1,0:T(2,128)} %param.7) | copy-start | bytes 388
  5.5 39.7 %all-to-all-start = ((bf16[64,12,128]{2,1,0:T(8,128)(2,1)}), bf16[64,12,128]{2,1,0:T(8,128)(2,1)S(1)}, u32[]{:S(2)}, u32[]{:S(2)}) async-start(bf16[64,12,128]{2,1,0:T(8,128)(2,1)} %pack.1), calls=%async_computation | async-start | bytes 524288 | tf_op jit(solution)/shard_map/all_to_all | solution.py:138
  24.4 34.2 %copy-start = (s32[512,1024]{1,0:T(8,128)S(1)}, s32[512,1024]{1,0:T(8,128)}, u32[]{:S(2)}) copy-start(s32[512,1024]{1,0:T(8,128)} %live_ref.3) | copy-start | bytes 6291460
  26.0 32.6 %collective-permute-start = (bf16[256,2048]{1,0:T(8,128)(2,1)S(1)}, bf16[256,2048]{1,0:T(8,128)(2,1)}, u32[]{:S(2)}, u32[]{:S(2)}) collective-permute-start(bf16[256,2048]{1,0:T(8,128)(2,1)S(1)} %bitcast_multiply_fusion.own_ref), channel_id=1, source_target_pairs={{0,1},{1,0},{2,3},{3,2},{4,5},{5,4},{6,7},{7,6},{8,9},{9,8},{10,11... | collective-permute-start | bytes 3145736 | tf_op jit(solution)/shard_map/ppermute | solution.py:136

commit v2 on v1

--- a/solution.py
+++ b/solution.py
@@ -48,13 +48,15 @@
         dropped = (is_dead > 0.5) & (count < DROP - 0.5)
         key = jnp.where(dropped, -1.0, tile - jnp.minimum(count, float(DROP)))
         pick = jnp.where(slot == key, 1.0, 0.0).astype(BF16)
-        packed = dot(pick, amp_ref[q * lanes : (q + 1) * lanes, :]).astype(BF16)
+        part = amp_ref[:, q * lanes * TW : (q + 1) * lanes * TW]
+        tiles = part.astype(F32).reshape(lanes, TW).astype(BF16)
+        packed = dot(pick, tiles).astype(BF16)
         for i in range(16):
             z, y = q * 4 + i // NY, i % NY
             out_ref[y * NZ + z] = packed[i * CT : i * CT + CAP, :]
 
 
-def pack(me, live, amp_tiles):
+def pack(me, live, amplitudes):
     return pl.pallas_call(
         pack_kernel,
         out_shape=jax.ShapeDtypeStruct((NW, CAP, TW), BF16),
@@ -63,15 +65,19 @@
             grid=(1,),
             in_specs=[
                 pl.BlockSpec((8, NW * CT), lambda i, me: (me[0] // 8, 0)),
-                pl.BlockSpec((NW * CT, TW), lambda i, me: (0, 0)),
+                pl.BlockSpec((1, NW * CT * TW), lambda i, me: (0, 0)),
             ],
             out_specs=pl.BlockSpec((NW, CAP, TW), lambda i, me: (0, 0, 0)),
         ),
         name="pack",
-    )(me, live, amp_tiles)
+    )(me, live, amplitudes)
 
 
-def ladder_kernel(ids_ref, live_ref, amp_ref, own_ref, other_ref, out_ref, used_ref):
+def whole(*dims):
+    return pl.BlockSpec(dims, lambda i, *ids: (0,) * len(dims))
+
+
+def codes_kernel(ids_ref, live_ref, out_ref):
     wide, core = ids_ref[0], ids_ref[1]
     rows = NX * NW
     r, g = iota((rows, 512), 0), iota((rows, 512), 1)
@@ -88,9 +94,28 @@
     code = jnp.where(here > 0.5, jnp.minimum(count, float(DROP)), 9.0).astype(BF16)
     spread_row, spread_col = iota((TW, CT * TW), 0), iota((TW, CT * TW), 1)
     spread = jnp.where(spread_row == spread_col // TW, 1.0, 0.0).astype(BF16)
-    codes = dot(code, spread).astype(BF16)
+    out_ref[...] = dot(code, spread).astype(BF16)
+
+
+def codes_of(ids, live):
+    return pl.pallas_call(
+        codes_kernel,
+        out_shape=jax.ShapeDtypeStruct((NX * NW, CT * TW), BF16),
+        grid_spec=pltpu.PrefetchScalarGridSpec(
+            num_scalar_prefetch=1,
+            grid=(1,),
+            in_specs=[pl.BlockSpec((512, TW), lambda i, ids: (0, ids[0] // 8))],
+            out_specs=whole(NX * NW, CT * TW),
+        ),
+        name="codes",
+    )(ids, live)
+
+
+def ladder_kernel(ids_ref, code_ref, amp_ref, own_ref, other_ref, out_ref, used_ref):
+    core = ids_ref[1]
+    rows = NX * NW
     for t in range(CT):
-        code_t = codes[:, t * TW : (t + 1) * TW]
+        code_t = code_ref[:, t * TW : (t + 1) * TW]
         value = jnp.zeros((rows, TW), BF16)
         for d in range(DROP + 1):
             if 0 <= t - d < CAP:
@@ -105,8 +130,7 @@
                 out_ref[y, column, x * NZ : (x + 1) * NZ, :] = sums[at : at + NZ, :]
 
 
-def ladder(ids, live, amp, own, other):
-    whole = lambda *dims: pl.BlockSpec(dims, lambda i, ids: (0,) * len(dims))
+def ladder(ids, codes, amp, own, other):
     return pl.pallas_call(
         ladder_kernel,
         out_shape=jax.ShapeDtypeStruct((NY, NC, NX * NZ, 256), F32),
@@ -114,7 +138,7 @@
             num_scalar_prefetch=1,
             grid=(1,),
             in_specs=[
-                pl.BlockSpec((512, TW), lambda i, ids: (0, ids[0] // 8)),
+                whole(NX * NW, CT * TW),
                 whole(CAP, NX * NW, TW),
                 whole(256, CT * TW),
                 whole(256, CT * TW),
@@ -124,7 +148,23 @@
         ),
         compiler_params=pltpu.CompilerParams(vmem_limit_bytes=40 * 1024 * 1024),
         name="ladder",
-    )(ids, live, amp, own, other)
+    )(ids, codes, amp, own, other)
+
+
+def finish_kernel(sums_ref, out_ref):
+    for x in range(NX):
+        total = jnp.sum(sums_ref[x * NZ : (x + 1) * NZ], axis=0).astype(BF16)
+        for c in range(NC):
+            at = (x * NC + c) * 256
+            out_ref[:, at : at + 256] = total[c : c + 1, :]
+
+
+def finish(sums):
+    return pl.pallas_call(
+        finish_kernel,
+        out_shape=jax.ShapeDtypeStruct((1, NX * NC * 256), BF16),
+        name="finish",
+    )(sums)
 
 
 def per_device(amplitudes, amplitude_live, integrals, integral_live):
@@ -134,13 +174,14 @@
     mask = integral_live.astype(BF16)
     own = (integrals.reshape(2, TW, CT, TW) * mask[:, None, :, None]).reshape(2 * TW, CT * TW)
     other = lax.ppermute(own, "c", [(0, 1), (1, 0)])
-    packed = pack(me.reshape(1), amplitude_live, amplitudes.reshape(NW * CT, TW))
+    packed = pack(me.reshape(1), amplitude_live, amplitudes)
     arrived = lax.all_to_all(packed, ("y", "z"), 0, 0, tiled=True)
     gathered = lax.all_gather(arrived.transpose(1, 0, 2), "x", axis=1, tiled=True)
-    sums = ladder(jnp.stack([wide, core]), amplitude_live, gathered, own, other)
+    ids = jnp.stack([wide, core])
+    sums = ladder(ids, codes_of(ids, amplitude_live), gathered, own, other)
     sums = lax.all_to_all(sums, "y", 0, 0, tiled=True).sum(axis=0)
     sums = lax.all_to_all(sums.transpose(1, 0, 2), ("x", "z"), 0, 0, tiled=True)
-    return sums.reshape(NX, NZ, NC * 256).sum(axis=1).reshape(1, NX * NC * 256).astype(BF16)
+    return finish(sums)
 
 
 def solution(mesh):

time: 96.3 us -> 92.6 us (0.962)
  other arithmetic: 4.94 us -> 0.92 us
  Pallas kernels: 5.49 us -> 9.02 us
  waiting for transfers between devices: 17.1 us -> 14.5 us
    pallas_call x0 -> x2, Pallas kernels: none -> 4.98 us  [the longest x1 3.42 us: codes_of(): pl.pallas_call(codes_kernel, out_shape=jax.ShapeDtypeStruct((NX * NW, CT...]
    unnamed x1 -> x0, other arithmetic: 3.18 us -> none
    all_to_all x1, waiting for transfers between devices: 17.1 us -> 14.5 us  [per_device(): arrived = lax.all_to_all(packed, ('y', 'z'), 0, 0, tiled=True)]
    pallas_call x1, Pallas kernels: 3.22 us -> 1.63 us  [ladder(): pl.pallas_call(ladder_kernel, out_shape=jax.ShapeDtypeStruct((NY, NC, NX...]
    mul x1, other arithmetic: 1.6 us -> 0.23 us  [per_device(): integrals.reshape(2, TW, CT, TW) * mask[:, None, :, None]]
  transfers between devices with their start and end apart: 2 -> 2, of which waited for: 1 -> 1; matrix products, arithmetic and copies ran while one was open for 2% -> 1% of each run, Pallas kernels for 0% -> 4%
where the time goes in v2:
time: 92.6 us; the launch traced here: 92.2 us
  blocking collectives  46.7 us (50%)
  starting transfers between devices  20.6 us (22%)
  waiting for transfers between devices  14.5 us (16%)
  Pallas kernels  9.02 us (10%)
    all_to_all x1, blocking collectives, per_device(): sums = lax.all_to_all(sums.transpose(1, 0, 2), ('x', 'z'), 0, 0, tiled=True)  21.2 us
    all_to_all x1, starting transfers between devices, per_device(): arrived = lax.all_to_all(packed, ('y', 'z'), 0, 0, tiled=True)  18.7 us
    all_to_all x1, waiting for transfers between devices, per_device(): arrived = lax.all_to_all(packed, ('y', 'z'), 0, 0, tiled=True)  14.5 us
    all_gather x1, blocking collectives, per_device(): lax.all_gather(arrived.transpose(1, 0, 2), 'x', axis=1, tiled=True)  13.4 us
    all_to_all x1, blocking collectives, per_device(): sums = lax.all_to_all(sums, 'y', 0, 0, tiled=True).sum(axis=0)  12.2 us
    pallas_call x1, Pallas kernels, codes_of(): pl.pallas_call(codes_kernel, out_shape=jax.ShapeDtypeStruct((NX * NW, CT...  3.42 us
    pallas_call x1, Pallas kernels, pack(): pl.pallas_call(pack_kernel, out_shape=jax.ShapeDtypeStruct((NW, CAP, TW),...  2.41 us
    ppermute x1, starting transfers between devices, per_device(): other = lax.ppermute(own, 'c', [(0, 1), (1, 0)])  1.92 us
  transfers between devices with their start and end apart: 2, of which 1 were waited for; matrix products, arithmetic and copies ran while one was open for 1% of the time, Pallas kernels for 4%

profile of v2, /device:TPU:2, one launch (start us, length us, event | category | flops | bytes accessed | tf_op | source)
XLA Modules:
  0.0 92.2 jit_solution(3077272361584208565)
XLA Ops:
  0.0 0.0 copy-start.3
  0.0 0.0 copy-start.2
  0.0 2.4 %pack.1 = bf16[64,12,128]{2,1,0:T(8,128)(2,1)} custom-call(s32[1]{0:T(128)} %bitcast.2.me_ref, s32[512,1024]{1,0:T(8,128)} %live_ref.3, bf16[1,131072]{1,0:T(2,128)(2,1)} %amp_ref.1), custom_call_target="tpu_custom_call" | custom-call | tf_op jit(solution)/shard_map/pack/pallas_call | solution.py:60
  2.4 18.7 %all-to-all-start = ((bf16[64,12,128]{2,1,0:T(8,128)(2,1)}), bf16[64,12,128]{2,1,0:T(8,128)(2,1)S(1)}, u32[]{:S(2)}, u32[]{:S(2)}) async-start(bf16[64,12,128]{2,1,0:T(8,128)(2,1)} %pack.1), calls=%async_computation | async-start | bytes 524288 | tf_op jit(solution)/shard_map/all_to_all | solution.py:178
  21.2 0.0 copy-done.3
  21.2 0.2 mul.23
  21.4 0.0 copy-done.2
  21.4 0.2 bitcast_multiply_fusion.own_ref
  21.6 1.9 %collective-permute-start = (bf16[256,2048]{1,0:T(8,128)(2,1)S(1)}, bf16[256,2048]{1,0:T(8,128)(2,1)S(1)}, u32[]{:S(2)}, u32[]{:S(2)}) collective-permute-start(bf16[256,2048]{1,0:T(8,128)(2,1)S(1)} %bitcast_multiply_fusion.own_ref), channel_id=1, source_target_pairs={{0,1},{1,0},{2,3},{3,2},{4,5},{5,4},{6,7},{7,6},{8,9},{9,8},{10,11... | collective-permute-start | bytes 3145736 | tf_op jit(solution)/shard_map/ppermute | solution.py:176
  23.6 0.7 pad_add_fusion.ids_ref
  24.2 0.0 copy-start.1
  24.2 3.4 %codes.1.code_ref = bf16[256,2048]{1,0:T(8,128)(2,1)} custom-call(s32[2]{0:T(128)} %pad_add_fusion.ids_ref, s32[512,1024]{1,0:T(8,128)} %live_ref.3), custom_call_target="tpu_custom_call" | custom-call | tf_op jit(solution)/shard_map/codes/pallas_call | solution.py:101
  27.6 0.0 copy-start
  27.6 14.5 %all-to-all-done = bf16[64,12,128]{2,1,0:T(8,128)(2,1)S(1)} async-done(((bf16[64,12,128]{2,1,0:T(8,128)(2,1)}), bf16[64,12,128]{2,1,0:T(8,128)(2,1)S(1)}, u32[]{:S(2)}, u32[]{:S(2)}) %all-to-all-start) | async-done | bytes 196640 | tf_op jit(solution)/shard_map/all_to_all | solution.py:178
  42.1 0.1 copy.12
  42.2 13.4 %all_gather.3.amp_ref = bf16[12,256,128]{2,1,0:T(8,128)(2,1)S(1)} all-gather(bf16[12,64,128]{2,1,0:T(8,128)(2,1)S(1)} %bitcast.14), channel_id=1, replica_groups=mesh['z'=16,'y'=4,'x'=4,'c'=2] {'x'}, dimensions={1}, use_global_device_ids=true | all-gather | bytes 983040 | tf_op jit(solution)/shard_map/all_gather | solution.py:179
  55.6 0.0 collective-permute-done.other_ref
  55.6 0.0 copy-done.1
  55.6 0.0 copy-done
  55.6 1.6 %ladder.1 = f32[4,2,64,256]{3,2,1,0:T(8,128)S(1)} custom-call(s32[2]{0:T(128)S(1)} %copy-done.1, bf16[256,2048]{1,0:T(8,128)(2,1)S(1)} %copy-done, bf16[12,256,128]{2,1,0:T(8,128)(2,1)S(1)} %all_gather.3.amp_ref, bf16[256,2048]{1,0:T(8,128)(2,1)S(1)} %bitcast_multiply_fusion.own_ref, bf16[256,2048]{1,0:T(8,128)(2,1)S(1)} %collective-permute-done.other_ref), custom_call_target="tpu_custom_call" | custom-call | tf_op jit(solution)/shard_map/ladder/pallas_call | solution.py:134
  57.2 12.2 %all_to_all.15 = f32[4,2,64,256]{3,2,1,0:T(8,128)S(1)} all-to-all(f32[4,2,64,256]{3,2,1,0:T(8,128)S(1)} %ladder.1), channel_id=1, replica_groups=mesh['z'=16,'y'=4,'x'=4,'c'=2] {'y'}, dimensions={0} | all-to-all | bytes 1048576 | tf_op jit(solution)/shard_map/all_to_all | solution.py:182
  69.4 0.1 copy.13
  69.5 21.2 %all_to_all.16.sums_ref = f32[64,2,256]{2,1,0:T(2,128)} all-to-all(f32[64,2,256]{2,1,0:T(2,128)S(1)} %bitcast.15), channel_id=1, replica_groups=mesh['z'=16,'y'=4,'x'=4,'c'=2] {'x','z'}, dimensions={0} | all-to-all | bytes 262144 | tf_op jit(solution)/shard_map/all_to_all | solution.py:183
  90.7 1.6 %finish.1 = bf16[1,2048]{1,0:T(2,128)(2,1)} custom-call(f32[64,2,256]{2,1,0:T(2,128)} %all_to_all.16.sums_ref), custom_call_target="tpu_custom_call" | custom-call | tf_op jit(solution)/shard_map/finish/pallas_call | solution.py:163
  (2 shorter events, 0.0 us)
Async XLA Ops:
  0.0 21.2 %copy-start.3 = (s32[2,16]{1,0:T(2,128)S(1)}, s32[2,16]{1,0:T(2,128)}, u32[]{:S(2)}) copy-start(s32[2,16]{1,0:T(2,128)} %param.7) | copy-start | bytes 388
  0.0 21.4 %copy-start.2 = (bf16[256,2048]{1,0:T(8,128)(2,1)S(1)}, bf16[256,2048]{1,0:T(8,128)(2,1)}, u32[]{:S(2)}) copy-start(bf16[256,2048]{1,0:T(8,128)(2,1)} %param.6) | copy-start | bytes 3145732
  2.4 39.7 %all-to-all-start = ((bf16[64,12,128]{2,1,0:T(8,128)(2,1)}), bf16[64,12,128]{2,1,0:T(8,128)(2,1)S(1)}, u32[]{:S(2)}, u32[]{:S(2)}) async-start(bf16[64,12,128]{2,1,0:T(8,128)(2,1)} %pack.1), calls=%async_computation | async-start | bytes 524288 | tf_op jit(solution)/shard_map/all_to_all | solution.py:178
  21.6 33.9 %collective-permute-start = (bf16[256,2048]{1,0:T(8,128)(2,1)S(1)}, bf16[256,2048]{1,0:T(8,128)(2,1)S(1)}, u32[]{:S(2)}, u32[]{:S(2)}) collective-permute-start(bf16[256,2048]{1,0:T(8,128)(2,1)S(1)} %bitcast_multiply_fusion.own_ref), channel_id=1, source_target_pairs={{0,1},{1,0},{2,3},{3,2},{4,5},{5,4},{6,7},{7,6},{8,9},{9,8},{10,11... | collective-permute-start | bytes 3145736 | tf_op jit(solution)/shard_map/ppermute | solution.py:176
  24.2 31.4 %copy-start.1 = (s32[2]{0:T(128)S(1)}, s32[2]{0:T(128)}, u32[]{:S(2)}) copy-start(s32[2]{0:T(128)} %pad_add_fusion.ids_ref) | copy-start | bytes 28
  27.6 27.9 %copy-start = (bf16[256,2048]{1,0:T(8,128)(2,1)S(1)}, bf16[256,2048]{1,0:T(8,128)(2,1)}, u32[]{:S(2)}) copy-start(bf16[256,2048]{1,0:T(8,128)(2,1)} %codes.1.code_ref) | copy-start | bytes 3145732

commit v3 on v2

--- a/solution.py
+++ b/solution.py
@@ -44,8 +44,7 @@
     for q in range(4):
         dead_q = dead[:, q * lanes : (q + 1) * lanes]
         count = jnp.concatenate([dot(dead_q[:, :TW], before), dot(dead_q[:, TW:], before)], axis=1)[0:1]
-        is_dead = dead_q[0:1].astype(F32)
-        dropped = (is_dead > 0.5) & (count < DROP - 0.5)
+        dropped = (row[:, q * lanes : (q + 1) * lanes] < 0.5) & (count < DROP - 0.5)
         key = jnp.where(dropped, -1.0, tile - jnp.minimum(count, float(DROP)))
         pick = jnp.where(slot == key, 1.0, 0.0).astype(BF16)
         part = amp_ref[:, q * lanes * TW : (q + 1) * lanes * TW]
@@ -53,13 +52,15 @@
         packed = dot(pick, tiles).astype(BF16)
         for i in range(16):
             z, y = q * 4 + i // NY, i % NY
-            out_ref[y * NZ + z] = packed[i * CT : i * CT + CAP, :]
+            for k in range(CAP // 4):
+                at = i * CT + k * 4
+                out_ref[y * NZ + z, :, k * TW : (k + 1) * TW] = packed[at : at + 4, :]
 
 
 def pack(me, live, amplitudes):
     return pl.pallas_call(
         pack_kernel,
-        out_shape=jax.ShapeDtypeStruct((NW, CAP, TW), BF16),
+        out_shape=jax.ShapeDtypeStruct((NW, 4, CAP // 4 * TW), BF16),
         grid_spec=pltpu.PrefetchScalarGridSpec(
             num_scalar_prefetch=1,
             grid=(1,),
@@ -67,7 +68,7 @@
                 pl.BlockSpec((8, NW * CT), lambda i, me: (me[0] // 8, 0)),
                 pl.BlockSpec((1, NW * CT * TW), lambda i, me: (0, 0)),
             ],
-            out_specs=pl.BlockSpec((NW, CAP, TW), lambda i, me: (0, 0, 0)),
+            out_specs=pl.BlockSpec((NW, 4, CAP // 4 * TW), lambda i, me: (0, 0, 0)),
         ),
         name="pack",
     )(me, live, amplitudes)
@@ -114,12 +115,13 @@
 def ladder_kernel(ids_ref, code_ref, amp_ref, own_ref, other_ref, out_ref, used_ref):
     core = ids_ref[1]
     rows = NX * NW
+    slots = [amp_ref[j % 4, :, j // 4 * TW : (j // 4 + 1) * TW] for j in range(CAP)]
     for t in range(CT):
         code_t = code_ref[:, t * TW : (t + 1) * TW]
         value = jnp.zeros((rows, TW), BF16)
         for d in range(DROP + 1):
             if 0 <= t - d < CAP:
-                value = jnp.where(code_t == d, amp_ref[t - d], value)
+                value = jnp.where(code_t == d, slots[t - d], value)
         used_ref[:, t * TW : (t + 1) * TW] = value
     used = used_ref[...]
     for ref, column in ((own_ref, core), (other_ref, 1 - core)):
@@ -127,44 +129,28 @@
         for y in range(NY):
             for x in range(NX):
                 at = x * NW + y * NZ
-                out_ref[y, column, x * NZ : (x + 1) * NZ, :] = sums[at : at + NZ, :]
+                out_ref[y * NX + x, column] = sums[at : at + NZ, :]
 
 
 def ladder(ids, codes, amp, own, other):
     return pl.pallas_call(
         ladder_kernel,
-        out_shape=jax.ShapeDtypeStruct((NY, NC, NX * NZ, 256), F32),
+        out_shape=jax.ShapeDtypeStruct((NY * NX, NC, NZ, 256), F32),
         grid_spec=pltpu.PrefetchScalarGridSpec(
             num_scalar_prefetch=1,
             grid=(1,),
             in_specs=[
                 whole(NX * NW, CT * TW),
-                whole(CAP, NX * NW, TW),
+                whole(4, NX * NW, CAP // 4 * TW),
                 whole(256, CT * TW),
                 whole(256, CT * TW),
             ],
-            out_specs=whole(NY, NC, NX * NZ, 256),
+            out_specs=whole(NY * NX, NC, NZ, 256),
             scratch_shapes=[pltpu.VMEM((NX * NW, CT * TW), BF16)],
         ),
         compiler_params=pltpu.CompilerParams(vmem_limit_bytes=40 * 1024 * 1024),
         name="ladder",
     )(ids, codes, amp, own, other)
-
-
-def finish_kernel(sums_ref, out_ref):
-    for x in range(NX):
-        total = jnp.sum(sums_ref[x * NZ : (x + 1) * NZ], axis=0).astype(BF16)
-        for c in range(NC):
-            at = (x * NC + c) * 256
-            out_ref[:, at : at + 256] = total[c : c + 1, :]
-
-
-def finish(sums):
-    return pl.pallas_call(
-        finish_kernel,
-        out_shape=jax.ShapeDtypeStruct((1, NX * NC * 256), BF16),
-        name="finish",
-    )(sums)
 
 
 def per_device(amplitudes, amplitude_live, integrals, integral_live):
@@ -176,12 +162,15 @@
     other = lax.ppermute(own, "c", [(0, 1), (1, 0)])
     packed = pack(me.reshape(1), amplitude_live, amplitudes)
     arrived = lax.all_to_all(packed, ("y", "z"), 0, 0, tiled=True)
-    gathered = lax.all_gather(arrived.transpose(1, 0, 2), "x", axis=1, tiled=True)
+    slots = arrived.transpose(1, 0, 2)
+    gathered = lax.all_gather(slots, "x", axis=1, tiled=True)
     ids = jnp.stack([wide, core])
     sums = ladder(ids, codes_of(ids, amplitude_live), gathered, own, other)
-    sums = lax.all_to_all(sums, "y", 0, 0, tiled=True).sum(axis=0)
-    sums = lax.all_to_all(sums.transpose(1, 0, 2), ("x", "z"), 0, 0, tiled=True)
-    return finish(sums)
+    sums = lax.all_to_all(sums, ("y", "x"), 0, 0, tiled=True)
+    sums = sums.reshape(NY, NX, NC, NZ, 256).sum(axis=0)
+    sums = sums.transpose(2, 0, 1, 3).reshape(NZ, 16, TW)
+    sums = lax.all_to_all(sums, "z", 0, 0, tiled=True).sum(axis=0)
+    return sums.astype(BF16).reshape(1, NX * NC * 256)
 
 
 def solution(mesh):

time: 92.6 us -> 88.4 us (0.955)
  the two profiles are of different devices: /device:TPU:2 before, /device:TPU:32 now
where the time goes in v3:
time: 88.4 us; the launch traced here: 88 us
  blocking collectives  46.8 us (53%)
  starting transfers between devices  20.3 us (23%)
  waiting for transfers between devices  11.4 us (13%)
  Pallas kernels  7.54 us (9%)
  local copies, waits for them, and re-layouts  1.06 us (1%)
    all_to_all x1, starting transfers between devices, per_device(): arrived = lax.all_to_all(packed, ('y', 'z'), 0, 0, tiled=True)  18.4 us
    all_to_all x1, blocking collectives, per_device(): sums = lax.all_to_all(sums, 'z', 0, 0, tiled=True).sum(axis=0)  16.5 us
    all_to_all x1, blocking collectives, per_device(): sums = lax.all_to_all(sums, ('y', 'x'), 0, 0, tiled=True)  15.8 us
    all_gather x1, blocking collectives, per_device(): gathered = lax.all_gather(slots, 'x', axis=1, tiled=True)  14.5 us
    all_to_all x1, waiting for transfers between devices, per_device(): arrived = lax.all_to_all(packed, ('y', 'z'), 0, 0, tiled=True)  11.4 us
    pallas_call x1, Pallas kernels, codes_of(): pl.pallas_call(codes_kernel, out_shape=jax.ShapeDtypeStruct((NX * NW, CT...  3.43 us
    pallas_call x1, Pallas kernels, pack(): pl.pallas_call(pack_kernel, out_shape=jax.ShapeDtypeStruct((NW, 4, CAP //...  2.4 us
    ppermute x1, starting transfers between devices, per_device(): other = lax.ppermute(own, 'c', [(0, 1), (1, 0)])  1.92 us
  transfers between devices with their start and end apart: 2, of which 1 were waited for; matrix products, arithmetic and copies ran while one was open for 1% of the time, Pallas kernels for 4%

profile of v3, /device:TPU:32, one launch (start us, length us, event | category | flops | bytes accessed | tf_op | source)
XLA Modules:
  0.0 88.0 jit_solution(18285609883856645416)
XLA Ops:
  0.0 0.0 copy-start.3
  0.0 0.0 copy-start.2
  0.0 2.4 %pack.1 = bf16[64,4,384]{2,1,0:T(4,128)(2,1)} custom-call(s32[1]{0:T(128)} %bitcast.2.me_ref, s32[512,1024]{1,0:T(8,128)} %live_ref.3, bf16[1,131072]{1,0:T(2,128)(2,1)} %amp_ref.1), custom_call_target="tpu_custom_call" | custom-call | tf_op jit(solution)/shard_map/pack/pallas_call | solution.py:61
  2.4 18.4 %all-to-all-start = ((bf16[64,4,384]{2,1,0:T(4,128)(2,1)}), bf16[64,4,384]{2,1,0:T(4,128)(2,1)S(1)}, u32[]{:S(2)}, u32[]{:S(2)}) async-start(bf16[64,4,384]{2,1,0:T(4,128)(2,1)} %pack.1), calls=%async_computation | async-start | bytes 393216 | tf_op jit(solution)/shard_map/all_to_all | solution.py:164
  20.8 0.0 copy-done.3
  20.8 0.2 mul.23
  21.0 0.0 copy-done.2
  21.0 0.2 bitcast_multiply_fusion.own_ref
  21.3 1.9 %collective-permute-start = (bf16[256,2048]{1,0:T(8,128)(2,1)S(1)}, bf16[256,2048]{1,0:T(8,128)(2,1)S(1)}, u32[]{:S(2)}, u32[]{:S(2)}) collective-permute-start(bf16[256,2048]{1,0:T(8,128)(2,1)S(1)} %bitcast_multiply_fusion.own_ref), channel_id=1, source_target_pairs={{0,1},{1,0},{2,3},{3,2},{4,5},{5,4},{6,7},{7,6},{8,9},{9,8},{10,11... | collective-permute-start | bytes 3145736 | tf_op jit(solution)/shard_map/ppermute | solution.py:162
  23.2 0.6 pad_add_fusion.ids_ref
  23.8 0.0 copy-start.1
  23.8 3.4 %codes.1.code_ref = bf16[256,2048]{1,0:T(8,128)(2,1)} custom-call(s32[2]{0:T(128)} %pad_add_fusion.ids_ref, s32[512,1024]{1,0:T(8,128)} %live_ref.3), custom_call_target="tpu_custom_call" | custom-call | tf_op jit(solution)/shard_map/codes/pallas_call | solution.py:102
  27.2 0.0 copy-start
  27.2 11.4 %all-to-all-done = bf16[64,4,384]{2,1,0:T(4,128)(2,1)S(1)} async-done(((bf16[64,4,384]{2,1,0:T(4,128)(2,1)}), bf16[64,4,384]{2,1,0:T(4,128)(2,1)S(1)}, u32[]{:S(2)}, u32[]{:S(2)}) %all-to-all-start) | async-done | bytes 196640 | tf_op jit(solution)/shard_map/all_to_all | solution.py:164
  38.6 14.5 %all_gather.3.amp_ref = bf16[4,256,384]{2,1,0:T(8,128)(2,1)S(1)} all-gather(bf16[4,64,384]{2,1,0:T(8,128)(2,1)S(1)} %bitcast.21), channel_id=1, replica_groups=mesh['z'=16,'y'=4,'x'=4,'c'=2] {'x'}, dimensions={1}, use_global_device_ids=true | all-gather | bytes 983040 | tf_op jit(solution)/shard_map/all_gather | solution.py:166
  53.1 0.0 collective-permute-done.other_ref
  53.1 0.0 copy-done.1
  53.1 0.0 copy-done
  53.1 1.7 %ladder.1 = f32[16,2,16,256]{3,2,1,0:T(8,128)S(1)} custom-call(s32[2]{0:T(128)S(1)} %copy-done.1, bf16[256,2048]{1,0:T(8,128)(2,1)S(1)} %copy-done, bf16[4,256,384]{2,1,0:T(8,128)(2,1)S(1)} %all_gather.3.amp_ref, bf16[256,2048]{1,0:T(8,128)(2,1)S(1)} %bitcast_multiply_fusion.own_ref, bf16[256,2048]{1,0:T(8,128)(2,1)S(1)} %collective-permute-done.other_ref), custom_call_target="tpu_custom_call" | custom-call | tf_op jit(solution)/shard_map/ladder/pallas_call | solution.py:136
  54.8 15.8 %all_to_all.15 = f32[16,2,16,256]{3,2,1,0:T(8,128)S(1)} all-to-all(f32[16,2,16,256]{3,2,1,0:T(8,128)S(1)} %ladder.1), channel_id=1, replica_groups=mesh['z'=16,'y'=4,'x'=4,'c'=2] {'y','x'}, dimensions={0} | all-to-all | bytes 1048576 | tf_op jit(solution)/shard_map/all_to_all | solution.py:169
  70.7 0.1 copy.8
  70.8 0.1 reshape.27
  70.9 16.5 %all_to_all.16 = f32[16,16,128]{2,1,0:T(8,128)S(1)} all-to-all(f32[16,16,128]{2,1,0:T(8,128)S(1)} %reshape.27), channel_id=1, replica_groups=mesh['z'=16,'y'=4,'x'=4,'c'=2] {'z'}, dimensions={0} | all-to-all | bytes 262144 | tf_op jit(solution)/shard_map/all_to_all | solution.py:172
  87.4 0.6 copy.15
  (4 shorter events, 0.1 us)
Async XLA Ops:
  0.0 20.8 %copy-start.3 = (s32[2,16]{1,0:T(2,128)S(1)}, s32[2,16]{1,0:T(2,128)}, u32[]{:S(2)}) copy-start(s32[2,16]{1,0:T(2,128)} %param.7) | copy-start | bytes 388
  0.0 21.0 %copy-start.2 = (bf16[256,2048]{1,0:T(8,128)(2,1)S(1)}, bf16[256,2048]{1,0:T(8,128)(2,1)}, u32[]{:S(2)}) copy-start(bf16[256,2048]{1,0:T(8,128)(2,1)} %param.6) | copy-start | bytes 3145732
  2.4 36.2 %all-to-all-start = ((bf16[64,4,384]{2,1,0:T(4,128)(2,1)}), bf16[64,4,384]{2,1,0:T(4,128)(2,1)S(1)}, u32[]{:S(2)}, u32[]{:S(2)}) async-start(bf16[64,4,384]{2,1,0:T(4,128)(2,1)} %pack.1), calls=%async_computation | async-start | bytes 393216 | tf_op jit(solution)/shard_map/all_to_all | solution.py:164
  21.3 31.8 %collective-permute-start = (bf16[256,2048]{1,0:T(8,128)(2,1)S(1)}, bf16[256,2048]{1,0:T(8,128)(2,1)S(1)}, u32[]{:S(2)}, u32[]{:S(2)}) collective-permute-start(bf16[256,2048]{1,0:T(8,128)(2,1)S(1)} %bitcast_multiply_fusion.own_ref), channel_id=1, source_target_pairs={{0,1},{1,0},{2,3},{3,2},{4,5},{5,4},{6,7},{7,6},{8,9},{9,8},{10,11... | collective-permute-start | bytes 3145736 | tf_op jit(solution)/shard_map/ppermute | solution.py:162
  23.8 29.3 %copy-start.1 = (s32[2]{0:T(128)S(1)}, s32[2]{0:T(128)}, u32[]{:S(2)}) copy-start(s32[2]{0:T(128)} %pad_add_fusion.ids_ref) | copy-start | bytes 28
  27.2 25.9 %copy-start = (bf16[256,2048]{1,0:T(8,128)(2,1)S(1)}, bf16[256,2048]{1,0:T(8,128)(2,1)}, u32[]{:S(2)}) copy-start(bf16[256,2048]{1,0:T(8,128)(2,1)} %codes.1.code_ref) | copy-start | bytes 3145732

commit v4 on v3

v4 whole, which is shorter than its diff:
```python
import functools

import jax
import jax.numpy as jnp
from jax import lax
from jax.experimental import pallas as pl
from jax.experimental.pallas import tpu as pltpu
from jax.sharding import Mesh, PartitionSpec as P

TW = 128
NZ, NY, NX, NC = 16, 4, 4, 2
NW = NZ * NY
CT = 16
CAP = 12
DROP = CT - CAP
F32 = jnp.float32
BF16 = jnp.bfloat16


def iota(shape, dim):
    return lax.broadcasted_iota(jnp.int32, shape, dim)


def dot(a, b):
    return lax.dot_general(a, b, (((1,), (0,)), ((), ())), preferred_element_type=F32)


def before_matrix():
    rows, cols = iota((TW, TW), 0), iota((TW, TW), 1)
    same = (rows >> 4) == (cols >> 4)
    return jnp.where(same & (rows < cols), 1.0, 0.0).astype(BF16)


def own_wide():
    return lax.axis_index("z") * NY + lax.axis_index("y")


def pack_kernel(live_ref, amp_ref, out_ref, live_in, amp_in, packed_out, live_sem, in_sem, out_sem):
    lanes = 2 * TW
    block = pl.multiple_of(own_wide() * 8, 8)
    fetch_live = pltpu.make_async_copy(live_ref.at[pl.ds(block, 8)], live_in, live_sem)
    fetch_live.start()
    fetch = [
        pltpu.make_async_copy(amp_ref.at[:, pl.ds(q * lanes * TW, lanes * TW)], amp_in.at[q], in_sem.at[q])
        for q in range(4)
    ]
    for copy in fetch:
        copy.start()
    before = before_matrix()
    out_row, col = iota((lanes, lanes), 0), iota((lanes, lanes), 1)
    slot = jnp.where(out_row >> 4 == col >> 4, out_row & 15, -7).astype(F32)
    tile = (iota((1, lanes), 1) & 15).astype(F32)
    fetch_live.wait()
    live = live_in[...].astype(F32)
    sub = lax.axis_index("x") * NC + lax.axis_index("c")
    row = jnp.sum(jnp.where(iota(live.shape, 0) == sub, live, 0.0), axis=0, keepdims=True)
    dead = jnp.broadcast_to(1.0 - row, (8, NW * CT)).astype(BF16)
    blocks = jnp.concatenate([dead[:, j * TW : (j + 1) * TW] for j in range(8)], axis=0)
    counts = dot(blocks, before)
    picks = []
    for q in range(4):
        count = jnp.concatenate([counts[16 * q : 16 * q + 1], counts[16 * q + 8 : 16 * q + 9]], axis=1)
        dropped = (row[:, q * lanes : (q + 1) * lanes] < 0.5) & (count < DROP - 0.5)
        key = jnp.where(dropped, -1.0, tile - jnp.minimum(count, float(DROP)))
        picks.append(jnp.where(slot == key, 1.0, 0.0).astype(BF16))
    for copy in fetch:
        copy.wait()
    tiles = [amp_in[q].astype(F32).reshape(lanes, TW).astype(BF16) for q in range(4)]
    packs = [dot(picks[q], tiles[q]).astype(BF16) for q in range(4)]
    store = []
    for q in range(4):
        for i in range(16):
            for k in range(CAP // 4):
                at = i * CT + k * 4
                packed_out[q, i, :, k * TW : (k + 1) * TW] = packs[q][at : at + 4, :]
        copy = pltpu.make_async_copy(packed_out.at[q], out_ref.at[pl.ds(q * 16, 16)], out_sem.at[q])
        copy.start()
        store.append(copy)
    for copy in store:
        copy.wait()


def pack(live, amplitudes):
    lanes = 2 * TW
    anywhere = pl.BlockSpec(memory_space=pl.ANY)
    return pl.pallas_call(
        pack_kernel,
        out_shape=jax.ShapeDtypeStruct((NW, 4, CAP // 4 * TW), BF16),
        in_specs=[anywhere, anywhere],
        out_specs=anywhere,
        scratch_shapes=[
            pltpu.VMEM((8, NW * CT), jnp.int32),
            pltpu.VMEM((4, 1, lanes * TW), BF16),
            pltpu.VMEM((4, 16, 4, CAP // 4 * TW), BF16),
            pltpu.SemaphoreType.DMA,
            pltpu.SemaphoreType.DMA((4,)),
            pltpu.SemaphoreType.DMA((4,)),
        ],
        name="pack",
    )(live, amplitudes)


def whole(*dims):
    return pl.BlockSpec(dims, lambda i, *ids: (0,) * len(dims))


def codes_kernel(ids_ref, live_ref, out_ref):
    wide, core = ids_ref[0], ids_ref[1]
    rows = NX * NW
    r, g = iota((rows, 512), 0), iota((rows, 512), 1)
    rx, ry, rz = r >> 6, (r >> 4) & 3, r & 15
    source = (rz << 5) + (ry << 3) + (rx << 1) + core
    pick = jnp.where(g == source, 1.0, 0.0).astype(BF16)
    live = dot(pick, live_ref[...].astype(F32).astype(BF16)).astype(BF16)
    base = (wide % 8) * CT
    lane, c = iota((TW, TW), 0), iota((TW, TW), 1)
    take = jnp.where((lane == base + c) & (c < CT), 1.0, 0.0).astype(BF16)
    prior = jnp.where((lane >= base) & (lane < base + c) & (c < CT), 1.0, 0.0).astype(BF16)
    here = dot(live, take)
    count = dot((1.0 - live.astype(F32)).astype(BF16), prior)
    code = jnp.where(here > 0.5, jnp.minimum(count, float(DROP)), 9.0).astype(BF16)
    spread_row, spread_col = iota((TW, CT * TW), 0), iota((TW, CT * TW), 1)
    spread = jnp.where(spread_row == spread_col // TW, 1.0, 0.0).astype(BF16)
    out_ref[...] = dot(code, spread).astype(BF16)


def codes_of(ids, live):
    return pl.pallas_call(
        codes_kernel,
        out_shape=jax.ShapeDtypeStruct((NX * NW, CT * TW), BF16),
        grid_spec=pltpu.PrefetchScalarGridSpec(
            num_scalar_prefetch=1,
            grid=(1,),
            in_specs=[pl.BlockSpec((512, TW), lambda i, ids: (0, ids[0] // 8))],
            out_specs=whole(NX * NW, CT * TW),
        ),
        name="codes",
    )(ids, live)


def ladder_kernel(code_ref, amp_ref, own_ref, other_ref, out_ref, used_ref):
    core = lax.axis_index("c")
    rows = NX * NW
    slots = [amp_ref[j % 4, :, j // 4 * TW : (j // 4 + 1) * TW] for j in range(CAP)]
    for t in range(CT):
        code_t = code_ref[:, t * TW : (t + 1) * TW]
        value = jnp.zeros((rows, TW), BF16)
        for d in range(DROP + 1):
            if 0 <= t - d < CAP:
                value = jnp.where(code_t == d, slots[t - d], value)
        used_ref[:, t * TW : (t + 1) * TW] = value
    used = used_ref[...]
    for ref, column in ((own_ref, core), (other_ref, 1 - core)):
        sums = lax.dot_general(used, ref[...], (((1,), (1,)), ((), ())), preferred_element_type=F32)
        for i in range(NX * NY):
            out_ref[i, column] = sums[i * NZ : (i + 1) * NZ, :]


def ladder(codes, amp, own, other):
    return pl.pallas_call(
        ladder_kernel,
        out_shape=jax.ShapeDtypeStruct((NY * NX, NC, NZ, 256), F32),
        scratch_shapes=[pltpu.VMEM((NX * NW, CT * TW), BF16)],
        compiler_params=pltpu.CompilerParams(vmem_limit_bytes=40 * 1024 * 1024),
        name="ladder",
    )(codes, amp, own, other)


def per_device(amplitudes, amplitude_live, integrals, integral_live):
    mask = integral_live.astype(BF16)
    own = (integrals.reshape(2, TW, CT, TW) * mask[:, None, :, None]).reshape(2 * TW, CT * TW)
    other = lax.ppermute(own, "c", [(0, 1), (1, 0)])
    packed = pack(amplitude_live, amplitudes)
    arrived = lax.all_to_all(packed, ("z", "y"), 0, 0, tiled=True)
    slots = arrived.reshape(NZ, NY, 4, CAP // 4 * TW).transpose(2, 1, 0, 3).reshape(4, NW, CAP // 4 * TW)
    gathered = lax.all_gather(slots, "x", axis=1, tiled=True)
    ids = jnp.stack([own_wide(), lax.axis_index("c")])
    sums = ladder(codes_of(ids, amplitude_live), gathered, own, other)
    sums = lax.all_to_all(sums, ("x", "y"), 0, 0, tiled=True)
    sums = sums.reshape(NX, NY, NC, NZ, 256).sum(axis=1)
    sums = sums.transpose(2, 0, 1, 3).reshape(NZ, 16, TW)
    sums = lax.all_to_all(sums, "z", 0, 0, tiled=True).sum(axis=0)
    return sums.astype(BF16).reshape(1, NX * NC * 256)


def solution(mesh):
    fine = Mesh(mesh.devices.reshape(NZ, NY, NX, NC), ("z", "y", "x", "c"))
    wide, grp = ("z", "y"), ("x", "c")
    return jax.shard_map(
        per_device,
        mesh=fine,
        in_specs=(P(wide + grp, None), P(), P(grp, wide), P(grp, wide)),
        out_specs=P(wide + grp, None),
        check_vma=False,
    )
```

time: 88.4 us -> 87.6 us (level)
  waiting for transfers between devices: 11.4 us -> 12.7 us
  blocking collectives: 46.8 us -> 45.5 us
    all_to_all x1, blocking collectives: 15.8 us -> 14.1 us  [per_device(): sums = lax.all_to_all(sums, ('x', 'y'), 0, 0, tiled=True)]
    all_to_all x1, waiting for transfers between devices: 11.4 us -> 12.7 us  [per_device(): arrived = lax.all_to_all(packed, ('z', 'y'), 0, 0, tiled=True)]
where the time goes in v4:
time: 87.6 us; the launch traced here: 87.3 us
  blocking collectives  45.5 us (52%)
  starting transfers between devices  20.3 us (23%)
  waiting for transfers between devices  12.7 us (14%)
  Pallas kernels  6.67 us (8%)
  local copies, waits for them, and re-layouts  1.07 us (1%)
  other arithmetic  0.95 us (1%)
    all_to_all x1, starting transfers between devices, per_device(): arrived = lax.all_to_all(packed, ('z', 'y'), 0, 0, tiled=True)  18.4 us
    all_to_all x1, blocking collectives, per_device(): sums = lax.all_to_all(sums, 'z', 0, 0, tiled=True).sum(axis=0)  16.7 us
    all_gather x1, blocking collectives, per_device(): gathered = lax.all_gather(slots, 'x', axis=1, tiled=True)  14.7 us
    all_to_all x1, blocking collectives, per_device(): sums = lax.all_to_all(sums, ('x', 'y'), 0, 0, tiled=True)  14.1 us
    all_to_all x1, waiting for transfers between devices, per_device(): arrived = lax.all_to_all(packed, ('z', 'y'), 0, 0, tiled=True)  12.7 us
    pallas_call x1, Pallas kernels, codes_of(): pl.pallas_call(codes_kernel, out_shape=jax.ShapeDtypeStruct((NX * NW, CT...  3.29 us
    pallas_call x1, Pallas kernels, pack(): pl.pallas_call(pack_kernel, out_shape=jax.ShapeDtypeStruct((NW, 4, CAP //...  2.29 us
    ppermute x1, starting transfers between devices, per_device(): other = lax.ppermute(own, 'c', [(0, 1), (1, 0)])  1.92 us
  transfers between devices with their start and end apart: 2, of which 1 were waited for; matrix products, arithmetic and copies ran while one was open for 1% of the time, Pallas kernels for 4%

profile of v4, /device:TPU:32, one launch (start us, length us, event | category | flops | bytes accessed | tf_op | source)
XLA Modules:
  0.0 87.3 jit_solution(6116293997738700794)
XLA Ops:
  0.0 0.0 copy-start.2
  0.0 0.0 copy-start.1
  0.0 2.3 %pack.1 = bf16[64,4,384]{2,1,0:T(4,128)(2,1)} custom-call(s32[512,1024]{1,0:T(8,128)} %live_ref.3, bf16[1,131072]{1,0:T(2,128)(2,1)} %amp_ref.1), custom_call_target="tpu_custom_call" | custom-call | tf_op jit(solution)/shard_map/pack/pallas_call | solution.py:86
  2.3 18.4 %all-to-all-start = ((bf16[64,4,384]{2,1,0:T(4,128)(2,1)}), bf16[64,4,384]{2,1,0:T(4,128)(2,1)S(1)}, u32[]{:S(2)}, u32[]{:S(2)}) async-start(bf16[64,4,384]{2,1,0:T(4,128)(2,1)} %pack.1), calls=%async_computation | async-start | bytes 393216 | tf_op jit(solution)/shard_map/all_to_all | solution.py:174
  20.7 0.0 copy-done.2
  20.7 0.2 mul.15
  20.9 0.0 copy-done.1
  21.0 0.2 bitcast_multiply_fusion.own_ref
  21.2 1.9 %collective-permute-start = (bf16[256,2048]{1,0:T(8,128)(2,1)S(1)}, bf16[256,2048]{1,0:T(8,128)(2,1)S(1)}, u32[]{:S(2)}, u32[]{:S(2)}) collective-permute-start(bf16[256,2048]{1,0:T(8,128)(2,1)S(1)} %bitcast_multiply_fusion.own_ref), channel_id=1, source_target_pairs={{0,1},{1,0},{2,3},{3,2},{4,5},{5,4},{6,7},{7,6},{8,9},{9,8},{10,11... | collective-permute-start | bytes 3145736 | tf_op jit(solution)/shard_map/ppermute | solution.py:172
  23.1 0.7 pad_add_fusion.ids_ref
  23.8 3.3 %codes.1.code_ref = bf16[256,2048]{1,0:T(8,128)(2,1)} custom-call(s32[2]{0:T(128)} %pad_add_fusion.ids_ref, s32[512,1024]{1,0:T(8,128)} %live_ref.3), custom_call_target="tpu_custom_call" | custom-call | tf_op jit(solution)/shard_map/codes/pallas_call | solution.py:128
  27.1 0.0 copy-start
  27.1 12.7 %all-to-all-done = bf16[64,4,384]{2,1,0:T(4,128)(2,1)S(1)} async-done(((bf16[64,4,384]{2,1,0:T(4,128)(2,1)}), bf16[64,4,384]{2,1,0:T(4,128)(2,1)S(1)}, u32[]{:S(2)}, u32[]{:S(2)}) %all-to-all-start) | async-done | bytes 196640 | tf_op jit(solution)/shard_map/all_to_all | solution.py:174
  39.8 14.7 %all_gather.3.amp_ref = bf16[4,256,384]{2,1,0:T(8,128)(2,1)S(1)} all-gather(bf16[4,64,384]{2,1,0:T(8,128)(2,1)S(1)} %bitcast.22), channel_id=1, replica_groups=mesh['z'=16,'y'=4,'x'=4,'c'=2] {'x'}, dimensions={1}, use_global_device_ids=true | all-gather | bytes 983040 | tf_op jit(solution)/shard_map/all_gather | solution.py:176
  54.5 0.0 collective-permute-done.other_ref
  54.5 0.0 copy-done
  54.5 1.1 %ladder.1 = f32[16,2,16,256]{3,2,1,0:T(8,128)S(1)} custom-call(bf16[256,2048]{1,0:T(8,128)(2,1)S(1)} %copy-done, bf16[4,256,384]{2,1,0:T(8,128)(2,1)S(1)} %all_gather.3.amp_ref, bf16[256,2048]{1,0:T(8,128)(2,1)S(1)} %bitcast_multiply_fusion.own_ref, bf16[256,2048]{1,0:T(8,128)(2,1)S(1)} %collective-permute-done.other_ref), custom_call_target="tpu_custom_call" | custom-call | tf_op jit(solution)/shard_map/ladder/pallas_call | solution.py:160
  55.6 14.1 %all_to_all.15 = f32[16,2,16,256]{3,2,1,0:T(8,128)S(1)} all-to-all(f32[16,2,16,256]{3,2,1,0:T(8,128)S(1)} %ladder.1), channel_id=1, replica_groups=mesh['z'=16,'y'=4,'x'=4,'c'=2] {'x','y'}, dimensions={0} | all-to-all | bytes 1048576 | tf_op jit(solution)/shard_map/all_to_all | solution.py:179
  69.8 0.1 copy.8
  69.9 0.1 reshape.31
  70.0 16.7 %all_to_all.16 = f32[16,16,128]{2,1,0:T(8,128)S(1)} all-to-all(f32[16,16,128]{2,1,0:T(8,128)S(1)} %reshape.31), channel_id=1, replica_groups=mesh['z'=16,'y'=4,'x'=4,'c'=2] {'z'}, dimensions={0} | all-to-all | bytes 262144 | tf_op jit(solution)/shard_map/all_to_all | solution.py:182
  86.7 0.6 copy.13
  (4 shorter events, 0.1 us)
Async XLA Ops:
  0.0 20.7 %copy-start.2 = (s32[2,16]{1,0:T(2,128)S(1)}, s32[2,16]{1,0:T(2,128)}, u32[]{:S(2)}) copy-start(s32[2,16]{1,0:T(2,128)} %param.7) | copy-start | bytes 388
  0.0 20.9 %copy-start.1 = (bf16[256,2048]{1,0:T(8,128)(2,1)S(1)}, bf16[256,2048]{1,0:T(8,128)(2,1)}, u32[]{:S(2)}) copy-start(bf16[256,2048]{1,0:T(8,128)(2,1)} %param.6) | copy-start | bytes 3145732
  2.3 37.5 %all-to-all-start = ((bf16[64,4,384]{2,1,0:T(4,128)(2,1)}), bf16[64,4,384]{2,1,0:T(4,128)(2,1)S(1)}, u32[]{:S(2)}, u32[]{:S(2)}) async-start(bf16[64,4,384]{2,1,0:T(4,128)(2,1)} %pack.1), calls=%async_computation | async-start | bytes 393216 | tf_op jit(solution)/shard_map/all_to_all | solution.py:174
  21.2 33.3 %collective-permute-start = (bf16[256,2048]{1,0:T(8,128)(2,1)S(1)}, bf16[256,2048]{1,0:T(8,128)(2,1)S(1)}, u32[]{:S(2)}, u32[]{:S(2)}) collective-permute-start(bf16[256,2048]{1,0:T(8,128)(2,1)S(1)} %bitcast_multiply_fusion.own_ref), channel_id=1, source_target_pairs={{0,1},{1,0},{2,3},{3,2},{4,5},{5,4},{6,7},{7,6},{8,9},{9,8},{10,11... | collective-permute-start | bytes 3145736 | tf_op jit(solution)/shard_map/ppermute | solution.py:172
  27.1 27.5 %copy-start = (bf16[256,2048]{1,0:T(8,128)(2,1)S(1)}, bf16[256,2048]{1,0:T(8,128)(2,1)}, u32[]{:S(2)}) copy-start(bf16[256,2048]{1,0:T(8,128)(2,1)} %codes.1.code_ref) | copy-start | bytes 3145732

commit v5 on v4

--- a/solution.py
+++ b/solution.py
@@ -35,17 +35,13 @@
     return lax.axis_index("z") * NY + lax.axis_index("y")
 
 
-def pack_kernel(live_ref, amp_ref, out_ref, live_in, amp_in, packed_out, live_sem, in_sem, out_sem):
+def pack_kernel(live_ref, amp_ref, out_ref, live_in, amp_in, packed_out, live_sem, amp_sem, out_sem):
     lanes = 2 * TW
     block = pl.multiple_of(own_wide() * 8, 8)
     fetch_live = pltpu.make_async_copy(live_ref.at[pl.ds(block, 8)], live_in, live_sem)
     fetch_live.start()
-    fetch = [
-        pltpu.make_async_copy(amp_ref.at[:, pl.ds(q * lanes * TW, lanes * TW)], amp_in.at[q], in_sem.at[q])
-        for q in range(4)
-    ]
-    for copy in fetch:
-        copy.start()
+    fetch_amp = pltpu.make_async_copy(amp_ref, amp_in, amp_sem)
+    fetch_amp.start()
     before = before_matrix()
     out_row, col = iota((lanes, lanes), 0), iota((lanes, lanes), 1)
     slot = jnp.where(out_row >> 4 == col >> 4, out_row & 15, -7).astype(F32)
@@ -63,9 +59,8 @@
         dropped = (row[:, q * lanes : (q + 1) * lanes] < 0.5) & (count < DROP - 0.5)
         key = jnp.where(dropped, -1.0, tile - jnp.minimum(count, float(DROP)))
         picks.append(jnp.where(slot == key, 1.0, 0.0).astype(BF16))
-    for copy in fetch:
-        copy.wait()
-    tiles = [amp_in[q].astype(F32).reshape(lanes, TW).astype(BF16) for q in range(4)]
+    fetch_amp.wait()
+    tiles = [amp_in[:, q * lanes * TW : (q + 1) * lanes * TW].astype(F32).reshape(lanes, TW).astype(BF16) for q in range(4)]
     packs = [dot(picks[q], tiles[q]).astype(BF16) for q in range(4)]
     store = []
     for q in range(4):
@@ -90,10 +85,10 @@
         out_specs=anywhere,
         scratch_shapes=[
             pltpu.VMEM((8, NW * CT), jnp.int32),
-            pltpu.VMEM((4, 1, lanes * TW), BF16),
+            pltpu.VMEM((1, NW * CT * TW), BF16),
             pltpu.VMEM((4, 16, 4, CAP // 4 * TW), BF16),
             pltpu.SemaphoreType.DMA,
-            pltpu.SemaphoreType.DMA((4,)),
+            pltpu.SemaphoreType.DMA,
             pltpu.SemaphoreType.DMA((4,)),
         ],
         name="pack",
@@ -141,7 +136,10 @@
 def ladder_kernel(code_ref, amp_ref, own_ref, other_ref, out_ref, used_ref):
     core = lax.axis_index("c")
     rows = NX * NW
-    slots = [amp_ref[j % 4, :, j // 4 * TW : (j // 4 + 1) * TW] for j in range(CAP)]
+    slots = [
+        jnp.concatenate([amp_ref[x * 4 + j % 4, :, j // 4 * TW : (j // 4 + 1) * TW] for x in range(NX)])
+        for j in range(CAP)
+    ]
     for t in range(CT):
         code_t = code_ref[:, t * TW : (t + 1) * TW]
         value = jnp.zeros((rows, TW), BF16)
@@ -173,14 +171,15 @@
     packed = pack(amplitude_live, amplitudes)
     arrived = lax.all_to_all(packed, ("z", "y"), 0, 0, tiled=True)
     slots = arrived.reshape(NZ, NY, 4, CAP // 4 * TW).transpose(2, 1, 0, 3).reshape(4, NW, CAP // 4 * TW)
-    gathered = lax.all_gather(slots, "x", axis=1, tiled=True)
+    gathered = lax.all_gather(slots, "x", axis=0, tiled=True)
     ids = jnp.stack([own_wide(), lax.axis_index("c")])
     sums = ladder(codes_of(ids, amplitude_live), gathered, own, other)
     sums = lax.all_to_all(sums, ("x", "y"), 0, 0, tiled=True)
     sums = sums.reshape(NX, NY, NC, NZ, 256).sum(axis=1)
     sums = sums.transpose(2, 0, 1, 3).reshape(NZ, 16, TW)
     sums = lax.all_to_all(sums, "z", 0, 0, tiled=True).sum(axis=0)
-    return sums.astype(BF16).reshape(1, NX * NC * 256)
+    sums = lax.optimization_barrier(sums.reshape(1, NX * NC * 256))
+    return sums.astype(BF16)
 
 
 def solution(mesh):

time: 87.6 us -> 87.5 us (level)
  no operation moved by 1% of the time
where the time goes in v5:
time: 87.5 us; the launch traced here: 87.2 us
  blocking collectives  45.5 us (52%)
  starting transfers between devices  20.3 us (23%)
  waiting for transfers between devices  12.7 us (15%)
  Pallas kernels  6.53 us (7%)
  other arithmetic  1.56 us (2%)
    all_to_all x1, starting transfers between devices, per_device(): arrived = lax.all_to_all(packed, ('z', 'y'), 0, 0, tiled=True)  18.4 us
    all_to_all x1, blocking collectives, per_device(): sums = lax.all_to_all(sums, 'z', 0, 0, tiled=True).sum(axis=0)  16.6 us
    all_gather x1, blocking collectives, per_device(): gathered = lax.all_gather(slots, 'x', axis=0, tiled=True)  14.7 us
    all_to_all x1, blocking collectives, per_device(): sums = lax.all_to_all(sums, ('x', 'y'), 0, 0, tiled=True)  14.1 us
    all_to_all x1, waiting for transfers between devices, per_device(): arrived = lax.all_to_all(packed, ('z', 'y'), 0, 0, tiled=True)  12.7 us
    pallas_call x1, Pallas kernels, codes_of(): pl.pallas_call(codes_kernel, out_shape=jax.ShapeDtypeStruct((NX * NW, CT...  3.29 us
    pallas_call x1, Pallas kernels, pack(): pl.pallas_call(pack_kernel, out_shape=jax.ShapeDtypeStruct((NW, 4, CAP //...  2.17 us
    ppermute x1, starting transfers between devices, per_device(): other = lax.ppermute(own, 'c', [(0, 1), (1, 0)])  1.92 us
  transfers between devices with their start and end apart: 2, of which 1 were waited for; matrix products, arithmetic and copies ran while one was open for 1% of the time, Pallas kernels for 4%

profile of v5, /device:TPU:32, one launch (start us, length us, event | category | flops | bytes accessed | tf_op | source)
XLA Modules:
  0.0 87.2 jit_solution(13676706902672769185)
XLA Ops:
  0.0 0.0 copy-start.2
  0.0 0.0 copy-start.1
  0.0 2.2 %pack.1 = bf16[64,4,384]{2,1,0:T(4,128)(2,1)} custom-call(s32[512,1024]{1,0:T(8,128)} %live_ref.3, bf16[1,131072]{1,0:T(2,128)(2,1)} %amp_ref.1), custom_call_target="tpu_custom_call" | custom-call | tf_op jit(solution)/shard_map/pack/pallas_call | solution.py:81
  2.2 18.4 %all-to-all-start = ((bf16[64,4,384]{2,1,0:T(4,128)(2,1)}), bf16[64,4,384]{2,1,0:T(4,128)(2,1)S(1)}, u32[]{:S(2)}, u32[]{:S(2)}) async-start(bf16[64,4,384]{2,1,0:T(4,128)(2,1)} %pack.1), calls=%async_computation | async-start | bytes 393216 | tf_op jit(solution)/shard_map/all_to_all | solution.py:172
  20.6 0.0 copy-done.2
  20.6 0.2 mul.15
  20.8 0.0 copy-done.1
  20.8 0.2 bitcast_multiply_fusion.own_ref
  21.1 1.9 %collective-permute-start = (bf16[256,2048]{1,0:T(8,128)(2,1)S(1)}, bf16[256,2048]{1,0:T(8,128)(2,1)S(1)}, u32[]{:S(2)}, u32[]{:S(2)}) collective-permute-start(bf16[256,2048]{1,0:T(8,128)(2,1)S(1)} %bitcast_multiply_fusion.own_ref), channel_id=1, source_target_pairs={{0,1},{1,0},{2,3},{3,2},{4,5},{5,4},{6,7},{7,6},{8,9},{9,8},{10,11... | collective-permute-start | bytes 3145736 | tf_op jit(solution)/shard_map/ppermute | solution.py:170
  23.0 0.7 pad_add_fusion.ids_ref
  23.7 3.3 %codes.1.code_ref = bf16[256,2048]{1,0:T(8,128)(2,1)} custom-call(s32[2]{0:T(128)} %pad_add_fusion.ids_ref, s32[512,1024]{1,0:T(8,128)} %live_ref.3), custom_call_target="tpu_custom_call" | custom-call | tf_op jit(solution)/shard_map/codes/pallas_call | solution.py:123
  27.0 0.0 copy-start
  27.0 12.7 %all-to-all-done = bf16[64,4,384]{2,1,0:T(4,128)(2,1)S(1)} async-done(((bf16[64,4,384]{2,1,0:T(4,128)(2,1)}), bf16[64,4,384]{2,1,0:T(4,128)(2,1)S(1)}, u32[]{:S(2)}, u32[]{:S(2)}) %all-to-all-start) | async-done | bytes 196640 | tf_op jit(solution)/shard_map/all_to_all | solution.py:172
  39.7 14.7 %all_gather.3.amp_ref = bf16[16,64,384]{2,1,0:T(8,128)(2,1)S(1)} all-gather(bf16[4,64,384]{2,1,0:T(8,128)(2,1)S(1)} %bitcast.16), channel_id=1, replica_groups=mesh['z'=16,'y'=4,'x'=4,'c'=2] {'x'}, dimensions={0}, use_global_device_ids=true | all-gather | bytes 983040 | tf_op jit(solution)/shard_map/all_gather | solution.py:174
  54.4 0.0 collective-permute-done.other_ref
  54.4 0.0 copy-done
  54.4 1.1 %ladder.1 = f32[16,2,16,256]{3,2,1,0:T(8,128)S(1)} custom-call(bf16[256,2048]{1,0:T(8,128)(2,1)S(1)} %copy-done, bf16[16,64,384]{2,1,0:T(8,128)(2,1)S(1)} %all_gather.3.amp_ref, bf16[256,2048]{1,0:T(8,128)(2,1)S(1)} %bitcast_multiply_fusion.own_ref, bf16[256,2048]{1,0:T(8,128)(2,1)S(1)} %collective-permute-done.other_ref), custom_call_target="tpu_custom_call" | custom-call | tf_op jit(solution)/shard_map/ladder/pallas_call | solution.py:158
  55.5 14.1 %all_to_all.15 = f32[16,2,16,256]{3,2,1,0:T(8,128)S(1)} all-to-all(f32[16,2,16,256]{3,2,1,0:T(8,128)S(1)} %ladder.1), channel_id=1, replica_groups=mesh['z'=16,'y'=4,'x'=4,'c'=2] {'x','y'}, dimensions={0} | all-to-all | bytes 1048576 | tf_op jit(solution)/shard_map/all_to_all | solution.py:177
  69.7 0.1 copy.8
  69.8 0.1 reshape.22
  69.9 16.6 %all_to_all.16 = f32[16,16,128]{2,1,0:T(8,128)S(1)} all-to-all(f32[16,16,128]{2,1,0:T(8,128)S(1)} %reshape.22), channel_id=1, replica_groups=mesh['z'=16,'y'=4,'x'=4,'c'=2] {'z'}, dimensions={0} | all-to-all | bytes 262144 | tf_op jit(solution)/shard_map/all_to_all | solution.py:180
  86.5 0.6 convert_element_type.7
  (4 shorter events, 0.1 us)
Async XLA Ops:
  0.0 20.6 %copy-start.2 = (s32[2,16]{1,0:T(2,128)S(1)}, s32[2,16]{1,0:T(2,128)}, u32[]{:S(2)}) copy-start(s32[2,16]{1,0:T(2,128)} %param.7) | copy-start | bytes 388
  0.0 20.8 %copy-start.1 = (bf16[256,2048]{1,0:T(8,128)(2,1)S(1)}, bf16[256,2048]{1,0:T(8,128)(2,1)}, u32[]{:S(2)}) copy-start(bf16[256,2048]{1,0:T(8,128)(2,1)} %param.6) | copy-start | bytes 3145732
  2.2 37.5 %all-to-all-start = ((bf16[64,4,384]{2,1,0:T(4,128)(2,1)}), bf16[64,4,384]{2,1,0:T(4,128)(2,1)S(1)}, u32[]{:S(2)}, u32[]{:S(2)}) async-start(bf16[64,4,384]{2,1,0:T(4,128)(2,1)} %pack.1), calls=%async_computation | async-start | bytes 393216 | tf_op jit(solution)/shard_map/all_to_all | solution.py:172
  21.1 33.3 %collective-permute-start = (bf16[256,2048]{1,0:T(8,128)(2,1)S(1)}, bf16[256,2048]{1,0:T(8,128)(2,1)S(1)}, u32[]{:S(2)}, u32[]{:S(2)}) collective-permute-start(bf16[256,2048]{1,0:T(8,128)(2,1)S(1)} %bitcast_multiply_fusion.own_ref), channel_id=1, source_target_pairs={{0,1},{1,0},{2,3},{3,2},{4,5},{5,4},{6,7},{7,6},{8,9},{9,8},{10,11... | collective-permute-start | bytes 3145736 | tf_op jit(solution)/shard_map/ppermute | solution.py:170
  27.0 27.5 %copy-start = (bf16[256,2048]{1,0:T(8,128)(2,1)S(1)}, bf16[256,2048]{1,0:T(8,128)(2,1)}, u32[]{:S(2)}) copy-start(bf16[256,2048]{1,0:T(8,128)(2,1)} %codes.1.code_ref) | copy-start | bytes 3145732

commit v6 on v5

--- a/solution.py
+++ b/solution.py
@@ -62,17 +62,14 @@
     fetch_amp.wait()
     tiles = [amp_in[:, q * lanes * TW : (q + 1) * lanes * TW].astype(F32).reshape(lanes, TW).astype(BF16) for q in range(4)]
     packs = [dot(picks[q], tiles[q]).astype(BF16) for q in range(4)]
-    store = []
     for q in range(4):
         for i in range(16):
             for k in range(CAP // 4):
                 at = i * CT + k * 4
-                packed_out[q, i, :, k * TW : (k + 1) * TW] = packs[q][at : at + 4, :]
-        copy = pltpu.make_async_copy(packed_out.at[q], out_ref.at[pl.ds(q * 16, 16)], out_sem.at[q])
-        copy.start()
-        store.append(copy)
-    for copy in store:
-        copy.wait()
+                packed_out[q * 16 + i, :, k * TW : (k + 1) * TW] = packs[q][at : at + 4, :]
+    store = pltpu.make_async_copy(packed_out, out_ref, out_sem)
+    store.start()
+    store.wait()
 
 
 def pack(live, amplitudes):
@@ -86,10 +83,10 @@
         scratch_shapes=[
             pltpu.VMEM((8, NW * CT), jnp.int32),
             pltpu.VMEM((1, NW * CT * TW), BF16),
-            pltpu.VMEM((4, 16, 4, CAP // 4 * TW), BF16),
+            pltpu.VMEM((NW, 4, CAP // 4 * TW), BF16),
             pltpu.SemaphoreType.DMA,
             pltpu.SemaphoreType.DMA,
-            pltpu.SemaphoreType.DMA((4,)),
+            pltpu.SemaphoreType.DMA,
         ],
         name="pack",
     )(live, amplitudes)
@@ -133,32 +130,37 @@
     )(ids, live)
 
 
-def ladder_kernel(code_ref, amp_ref, own_ref, other_ref, out_ref, used_ref):
+def ladder_kernel(code_ref, amp_ref, own_ref, other_ref, out_ref):
     core = lax.axis_index("c")
     rows = NX * NW
     slots = [
         jnp.concatenate([amp_ref[x * 4 + j % 4, :, j // 4 * TW : (j // 4 + 1) * TW] for x in range(NX)])
         for j in range(CAP)
     ]
-    for t in range(CT):
-        code_t = code_ref[:, t * TW : (t + 1) * TW]
-        value = jnp.zeros((rows, TW), BF16)
-        for d in range(DROP + 1):
-            if 0 <= t - d < CAP:
-                value = jnp.where(code_t == d, slots[t - d], value)
-        used_ref[:, t * TW : (t + 1) * TW] = value
-    used = used_ref[...]
-    for ref, column in ((own_ref, core), (other_ref, 1 - core)):
-        sums = lax.dot_general(used, ref[...], (((1,), (1,)), ((), ())), preferred_element_type=F32)
+    sums = [None, None]
+    for first in range(0, CT, 2):
+        values = []
+        for t in (first, first + 1):
+            code_t = code_ref[:, t * TW : (t + 1) * TW]
+            value = jnp.zeros((rows, TW), BF16)
+            for d in range(DROP + 1):
+                if 0 <= t - d < CAP:
+                    value = jnp.where(code_t == d, slots[t - d], value)
+            values.append(value)
+        used = jnp.concatenate(values, axis=1)
+        for i, ref in enumerate((own_ref, other_ref)):
+            part = ref[:, first * TW : (first + 2) * TW]
+            more = lax.dot_general(used, part, (((1,), (1,)), ((), ())), preferred_element_type=F32)
+            sums[i] = more if sums[i] is None else sums[i] + more
+    for total, column in ((sums[0], core), (sums[1], 1 - core)):
         for i in range(NX * NY):
-            out_ref[i, column] = sums[i * NZ : (i + 1) * NZ, :]
+            out_ref[i, column] = total[i * NZ : (i + 1) * NZ, :]
 
 
 def ladder(codes, amp, own, other):
     return pl.pallas_call(
         ladder_kernel,
         out_shape=jax.ShapeDtypeStruct((NY * NX, NC, NZ, 256), F32),
-        scratch_shapes=[pltpu.VMEM((NX * NW, CT * TW), BF16)],
         compiler_params=pltpu.CompilerParams(vmem_limit_bytes=40 * 1024 * 1024),
         name="ladder",
     )(codes, amp, own, other)

time: 87.5 us -> 87.3 us (level)
  no operation moved by 1% of the time
where the time goes in v6:
time: 87.3 us; the launch traced here: 87 us
  blocking collectives  45.5 us (52%)
  starting transfers between devices  20.3 us (23%)
  waiting for transfers between devices  12.7 us (15%)
  Pallas kernels  6.36 us (7%)
  other arithmetic  1.56 us (2%)
    all_to_all x1, starting transfers between devices, per_device(): arrived = lax.all_to_all(packed, ('z', 'y'), 0, 0, tiled=True)  18.4 us
    all_to_all x1, blocking collectives, per_device(): sums = lax.all_to_all(sums, 'z', 0, 0, tiled=True).sum(axis=0)  16.7 us
    all_gather x1, blocking collectives, per_device(): gathered = lax.all_gather(slots, 'x', axis=0, tiled=True)  14.7 us
    all_to_all x1, blocking collectives, per_device(): sums = lax.all_to_all(sums, ('x', 'y'), 0, 0, tiled=True)  14.1 us
    all_to_all x1, waiting for transfers between devices, per_device(): arrived = lax.all_to_all(packed, ('z', 'y'), 0, 0, tiled=True)  12.7 us
    pallas_call x1, Pallas kernels, codes_of(): pl.pallas_call(codes_kernel, out_shape=jax.ShapeDtypeStruct((NX * NW, CT...  3.29 us
    pallas_call x1, Pallas kernels, pack(): pl.pallas_call(pack_kernel, out_shape=jax.ShapeDtypeStruct((NW, 4, CAP //...  2.17 us
    ppermute x1, starting transfers between devices, per_device(): other = lax.ppermute(own, 'c', [(0, 1), (1, 0)])  1.92 us
  transfers between devices with their start and end apart: 2, of which 1 were waited for; matrix products, arithmetic and copies ran while one was open for 1% of the time, Pallas kernels for 4%

profile of v6, /device:TPU:32, one launch (start us, length us, event | category | flops | bytes accessed | tf_op | source)
XLA Modules:
  0.0 87.0 jit_solution(3566332737753739151)
XLA Ops:
  0.0 0.0 copy-start.2
  0.0 0.0 copy-start.1
  0.0 2.2 %pack.1 = bf16[64,4,384]{2,1,0:T(4,128)(2,1)} custom-call(s32[512,1024]{1,0:T(8,128)} %live_ref.3, bf16[1,131072]{1,0:T(2,128)(2,1)} %amp_ref.1), custom_call_target="tpu_custom_call" | custom-call | tf_op jit(solution)/shard_map/pack/pallas_call | solution.py:78
  2.2 18.4 %all-to-all-start = ((bf16[64,4,384]{2,1,0:T(4,128)(2,1)}), bf16[64,4,384]{2,1,0:T(4,128)(2,1)S(1)}, u32[]{:S(2)}, u32[]{:S(2)}) async-start(bf16[64,4,384]{2,1,0:T(4,128)(2,1)} %pack.1), calls=%async_computation | async-start | bytes 393216 | tf_op jit(solution)/shard_map/all_to_all | solution.py:174
  20.6 0.0 copy-done.2
  20.6 0.2 mul.15
  20.8 0.0 copy-done.1
  20.8 0.2 bitcast_multiply_fusion.own_ref
  21.1 1.9 %collective-permute-start = (bf16[256,2048]{1,0:T(8,128)(2,1)S(1)}, bf16[256,2048]{1,0:T(8,128)(2,1)S(1)}, u32[]{:S(2)}, u32[]{:S(2)}) collective-permute-start(bf16[256,2048]{1,0:T(8,128)(2,1)S(1)} %bitcast_multiply_fusion.own_ref), channel_id=1, source_target_pairs={{0,1},{1,0},{2,3},{3,2},{4,5},{5,4},{6,7},{7,6},{8,9},{9,8},{10,11... | collective-permute-start | bytes 3145736 | tf_op jit(solution)/shard_map/ppermute | solution.py:172
  23.0 0.7 pad_add_fusion.ids_ref
  23.7 3.3 %codes.1.code_ref = bf16[256,2048]{1,0:T(8,128)(2,1)} custom-call(s32[2]{0:T(128)} %pad_add_fusion.ids_ref, s32[512,1024]{1,0:T(8,128)} %live_ref.3), custom_call_target="tpu_custom_call" | custom-call | tf_op jit(solution)/shard_map/codes/pallas_call | solution.py:120
  27.0 0.0 copy-start
  27.0 12.7 %all-to-all-done = bf16[64,4,384]{2,1,0:T(4,128)(2,1)S(1)} async-done(((bf16[64,4,384]{2,1,0:T(4,128)(2,1)}), bf16[64,4,384]{2,1,0:T(4,128)(2,1)S(1)}, u32[]{:S(2)}, u32[]{:S(2)}) %all-to-all-start) | async-done | bytes 196640 | tf_op jit(solution)/shard_map/all_to_all | solution.py:174
  39.7 14.7 %all_gather.3.amp_ref = bf16[16,64,384]{2,1,0:T(8,128)(2,1)S(1)} all-gather(bf16[4,64,384]{2,1,0:T(8,128)(2,1)S(1)} %bitcast.16), channel_id=1, replica_groups=mesh['z'=16,'y'=4,'x'=4,'c'=2] {'x'}, dimensions={0}, use_global_device_ids=true | all-gather | bytes 983040 | tf_op jit(solution)/shard_map/all_gather | solution.py:176
  54.4 0.0 collective-permute-done.other_ref
  54.4 0.0 copy-done
  54.4 0.9 %ladder.1 = f32[16,2,16,256]{3,2,1,0:T(8,128)S(1)} custom-call(bf16[256,2048]{1,0:T(8,128)(2,1)S(1)} %copy-done, bf16[16,64,384]{2,1,0:T(8,128)(2,1)S(1)} %all_gather.3.amp_ref, bf16[256,2048]{1,0:T(8,128)(2,1)S(1)} %bitcast_multiply_fusion.own_ref, bf16[256,2048]{1,0:T(8,128)(2,1)S(1)} %collective-permute-done.other_ref), custom_call_target="tpu_custom_call" | custom-call | tf_op jit(solution)/shard_map/ladder/pallas_call | solution.py:161
  55.3 14.1 %all_to_all.15 = f32[16,2,16,256]{3,2,1,0:T(8,128)S(1)} all-to-all(f32[16,2,16,256]{3,2,1,0:T(8,128)S(1)} %ladder.1), channel_id=1, replica_groups=mesh['z'=16,'y'=4,'x'=4,'c'=2] {'x','y'}, dimensions={0} | all-to-all | bytes 1048576 | tf_op jit(solution)/shard_map/all_to_all | solution.py:179
  69.5 0.1 copy.8
  69.6 0.1 reshape.22
  69.7 16.7 %all_to_all.16 = f32[16,16,128]{2,1,0:T(8,128)S(1)} all-to-all(f32[16,16,128]{2,1,0:T(8,128)S(1)} %reshape.22), channel_id=1, replica_groups=mesh['z'=16,'y'=4,'x'=4,'c'=2] {'z'}, dimensions={0} | all-to-all | bytes 262144 | tf_op jit(solution)/shard_map/all_to_all | solution.py:182
  86.4 0.6 convert_element_type.7
  (4 shorter events, 0.1 us)
Async XLA Ops:
  0.0 20.6 %copy-start.2 = (s32[2,16]{1,0:T(2,128)S(1)}, s32[2,16]{1,0:T(2,128)}, u32[]{:S(2)}) copy-start(s32[2,16]{1,0:T(2,128)} %param.7) | copy-start | bytes 388
  0.0 20.8 %copy-start.1 = (bf16[256,2048]{1,0:T(8,128)(2,1)S(1)}, bf16[256,2048]{1,0:T(8,128)(2,1)}, u32[]{:S(2)}) copy-start(bf16[256,2048]{1,0:T(8,128)(2,1)} %param.6) | copy-start | bytes 3145732
  2.2 37.5 %all-to-all-start = ((bf16[64,4,384]{2,1,0:T(4,128)(2,1)}), bf16[64,4,384]{2,1,0:T(4,128)(2,1)S(1)}, u32[]{:S(2)}, u32[]{:S(2)}) async-start(bf16[64,4,384]{2,1,0:T(4,128)(2,1)} %pack.1), calls=%async_computation | async-start | bytes 393216 | tf_op jit(solution)/shard_map/all_to_all | solution.py:174
  21.1 33.3 %collective-permute-start = (bf16[256,2048]{1,0:T(8,128)(2,1)S(1)}, bf16[256,2048]{1,0:T(8,128)(2,1)S(1)}, u32[]{:S(2)}, u32[]{:S(2)}) collective-permute-start(bf16[256,2048]{1,0:T(8,128)(2,1)S(1)} %bitcast_multiply_fusion.own_ref), channel_id=1, source_target_pairs={{0,1},{1,0},{2,3},{3,2},{4,5},{5,4},{6,7},{7,6},{8,9},{9,8},{10,11... | collective-permute-start | bytes 3145736 | tf_op jit(solution)/shard_map/ppermute | solution.py:172
  27.0 27.5 %copy-start = (bf16[256,2048]{1,0:T(8,128)(2,1)S(1)}, bf16[256,2048]{1,0:T(8,128)(2,1)}, u32[]{:S(2)}) copy-start(bf16[256,2048]{1,0:T(8,128)(2,1)} %codes.1.code_ref) | copy-start | bytes 3145732

commit v7 on v6

--- a/solution.py
+++ b/solution.py
@@ -154,13 +154,14 @@
             sums[i] = more if sums[i] is None else sums[i] + more
     for total, column in ((sums[0], core), (sums[1], 1 - core)):
         for i in range(NX * NY):
-            out_ref[i, column] = total[i * NZ : (i + 1) * NZ, :]
+            for h in range(2):
+                out_ref[i, column * 2 + h] = total[i * NZ : (i + 1) * NZ, h * TW : (h + 1) * TW]
 
 
 def ladder(codes, amp, own, other):
     return pl.pallas_call(
         ladder_kernel,
-        out_shape=jax.ShapeDtypeStruct((NY * NX, NC, NZ, 256), F32),
+        out_shape=jax.ShapeDtypeStruct((NY * NX, 2 * NC, NZ, TW), F32),
         compiler_params=pltpu.CompilerParams(vmem_limit_bytes=40 * 1024 * 1024),
         name="ladder",
     )(codes, amp, own, other)
@@ -177,8 +178,8 @@
     ids = jnp.stack([own_wide(), lax.axis_index("c")])
     sums = ladder(codes_of(ids, amplitude_live), gathered, own, other)
     sums = lax.all_to_all(sums, ("x", "y"), 0, 0, tiled=True)
-    sums = sums.reshape(NX, NY, NC, NZ, 256).sum(axis=1)
-    sums = sums.transpose(2, 0, 1, 3).reshape(NZ, 16, TW)
+    sums = sums.reshape(NX, NY, 2 * NC, NZ, TW).sum(axis=1)
+    sums = sums.reshape(16, NZ, TW).transpose(1, 0, 2)
     sums = lax.all_to_all(sums, "z", 0, 0, tiled=True).sum(axis=0)
     sums = lax.optimization_barrier(sums.reshape(1, NX * NC * 256))
     return sums.astype(BF16)

time: 87.3 us -> 87.1 us (level)
  no operation moved by 1% of the time
where the time goes in v7:
time: 87.1 us; the launch traced here: 86.8 us
  blocking collectives  45.5 us (52%)
  starting transfers between devices  20.3 us (23%)
  waiting for transfers between devices  12.7 us (15%)
  Pallas kernels  6.36 us (7%)
  other arithmetic  1.56 us (2%)
    all_to_all x1, starting transfers between devices, per_device(): arrived = lax.all_to_all(packed, ('z', 'y'), 0, 0, tiled=True)  18.4 us
    all_to_all x1, blocking collectives, per_device(): sums = lax.all_to_all(sums, 'z', 0, 0, tiled=True).sum(axis=0)  16.7 us
    all_gather x1, blocking collectives, per_device(): gathered = lax.all_gather(slots, 'x', axis=0, tiled=True)  14.7 us
    all_to_all x1, blocking collectives, per_device(): sums = lax.all_to_all(sums, ('x', 'y'), 0, 0, tiled=True)  14.1 us
    all_to_all x1, waiting for transfers between devices, per_device(): arrived = lax.all_to_all(packed, ('z', 'y'), 0, 0, tiled=True)  12.7 us
    pallas_call x1, Pallas kernels, codes_of(): pl.pallas_call(codes_kernel, out_shape=jax.ShapeDtypeStruct((NX * NW, CT...  3.29 us
    pallas_call x1, Pallas kernels, pack(): pl.pallas_call(pack_kernel, out_shape=jax.ShapeDtypeStruct((NW, 4, CAP //...  2.17 us
    ppermute x1, starting transfers between devices, per_device(): other = lax.ppermute(own, 'c', [(0, 1), (1, 0)])  1.92 us
  transfers between devices with their start and end apart: 2, of which 1 were waited for; matrix products, arithmetic and copies ran while one was open for 1% of the time, Pallas kernels for 4%

profile of v7, /device:TPU:32, one launch (start us, length us, event | category | flops | bytes accessed | tf_op | source)
XLA Modules:
  0.0 86.8 jit_solution(14518990457313796768)
XLA Ops:
  0.0 0.0 copy-start.2
  0.0 0.0 copy-start.1
  0.0 2.2 %pack.1 = bf16[64,4,384]{2,1,0:T(4,128)(2,1)} custom-call(s32[512,1024]{1,0:T(8,128)} %live_ref.3, bf16[1,131072]{1,0:T(2,128)(2,1)} %amp_ref.1), custom_call_target="tpu_custom_call" | custom-call | tf_op jit(solution)/shard_map/pack/pallas_call | solution.py:78
  2.2 18.4 %all-to-all-start = ((bf16[64,4,384]{2,1,0:T(4,128)(2,1)}), bf16[64,4,384]{2,1,0:T(4,128)(2,1)S(1)}, u32[]{:S(2)}, u32[]{:S(2)}) async-start(bf16[64,4,384]{2,1,0:T(4,128)(2,1)} %pack.1), calls=%async_computation | async-start | bytes 393216 | tf_op jit(solution)/shard_map/all_to_all | solution.py:175
  20.6 0.0 copy-done.2
  20.6 0.2 mul.15
  20.8 0.0 copy-done.1
  20.8 0.2 bitcast_multiply_fusion.own_ref
  21.1 1.9 %collective-permute-start = (bf16[256,2048]{1,0:T(8,128)(2,1)S(1)}, bf16[256,2048]{1,0:T(8,128)(2,1)S(1)}, u32[]{:S(2)}, u32[]{:S(2)}) collective-permute-start(bf16[256,2048]{1,0:T(8,128)(2,1)S(1)} %bitcast_multiply_fusion.own_ref), channel_id=1, source_target_pairs={{0,1},{1,0},{2,3},{3,2},{4,5},{5,4},{6,7},{7,6},{8,9},{9,8},{10,11... | collective-permute-start | bytes 3145736 | tf_op jit(solution)/shard_map/ppermute | solution.py:173
  23.0 0.7 pad_add_fusion.ids_ref
  23.7 3.3 %codes.1.code_ref = bf16[256,2048]{1,0:T(8,128)(2,1)} custom-call(s32[2]{0:T(128)} %pad_add_fusion.ids_ref, s32[512,1024]{1,0:T(8,128)} %live_ref.3), custom_call_target="tpu_custom_call" | custom-call | tf_op jit(solution)/shard_map/codes/pallas_call | solution.py:120
  27.0 0.0 copy-start
  27.0 12.7 %all-to-all-done = bf16[64,4,384]{2,1,0:T(4,128)(2,1)S(1)} async-done(((bf16[64,4,384]{2,1,0:T(4,128)(2,1)}), bf16[64,4,384]{2,1,0:T(4,128)(2,1)S(1)}, u32[]{:S(2)}, u32[]{:S(2)}) %all-to-all-start) | async-done | bytes 196640 | tf_op jit(solution)/shard_map/all_to_all | solution.py:175
  39.7 14.7 %all_gather.3.amp_ref = bf16[16,64,384]{2,1,0:T(8,128)(2,1)S(1)} all-gather(bf16[4,64,384]{2,1,0:T(8,128)(2,1)S(1)} %bitcast.19), channel_id=1, replica_groups=mesh['z'=16,'y'=4,'x'=4,'c'=2] {'x'}, dimensions={0}, use_global_device_ids=true | all-gather | bytes 983040 | tf_op jit(solution)/shard_map/all_gather | solution.py:177
  54.4 0.0 collective-permute-done.other_ref
  54.4 0.0 copy-done
  54.4 0.9 %ladder.1 = f32[16,4,16,128]{3,2,1,0:T(8,128)S(1)} custom-call(bf16[256,2048]{1,0:T(8,128)(2,1)S(1)} %copy-done, bf16[16,64,384]{2,1,0:T(8,128)(2,1)S(1)} %all_gather.3.amp_ref, bf16[256,2048]{1,0:T(8,128)(2,1)S(1)} %bitcast_multiply_fusion.own_ref, bf16[256,2048]{1,0:T(8,128)(2,1)S(1)} %collective-permute-done.other_ref), custom_call_target="tpu_custom_call" | custom-call | tf_op jit(solution)/shard_map/ladder/pallas_call | solution.py:162
  55.3 14.1 %all_to_all.15 = f32[16,4,16,128]{3,2,1,0:T(8,128)S(1)} all-to-all(f32[16,4,16,128]{3,2,1,0:T(8,128)S(1)} %ladder.1), channel_id=1, replica_groups=mesh['z'=16,'y'=4,'x'=4,'c'=2] {'x','y'}, dimensions={0} | all-to-all | bytes 1048576 | tf_op jit(solution)/shard_map/all_to_all | solution.py:180
  69.5 16.7 %all_to_all.16 = f32[16,16,128]{2,1,0:T(8,128)S(1)} all-to-all(f32[16,16,128]{2,1,0:T(8,128)S(1)} %bitcast.21), channel_id=1, replica_groups=mesh['z'=16,'y'=4,'x'=4,'c'=2] {'z'}, dimensions={0} | all-to-all | bytes 262144 | tf_op jit(solution)/shard_map/all_to_all | solution.py:183
  86.2 0.6 convert_element_type.7
  (5 shorter events, 0.1 us)
Async XLA Ops:
  0.0 20.6 %copy-start.2 = (s32[2,16]{1,0:T(2,128)S(1)}, s32[2,16]{1,0:T(2,128)}, u32[]{:S(2)}) copy-start(s32[2,16]{1,0:T(2,128)} %param.7) | copy-start | bytes 388
  0.0 20.8 %copy-start.1 = (bf16[256,2048]{1,0:T(8,128)(2,1)S(1)}, bf16[256,2048]{1,0:T(8,128)(2,1)}, u32[]{:S(2)}) copy-start(bf16[256,2048]{1,0:T(8,128)(2,1)} %param.6) | copy-start | bytes 3145732
  2.2 37.5 %all-to-all-start = ((bf16[64,4,384]{2,1,0:T(4,128)(2,1)}), bf16[64,4,384]{2,1,0:T(4,128)(2,1)S(1)}, u32[]{:S(2)}, u32[]{:S(2)}) async-start(bf16[64,4,384]{2,1,0:T(4,128)(2,1)} %pack.1), calls=%async_computation | async-start | bytes 393216 | tf_op jit(solution)/shard_map/all_to_all | solution.py:175
  21.1 33.3 %collective-permute-start = (bf16[256,2048]{1,0:T(8,128)(2,1)S(1)}, bf16[256,2048]{1,0:T(8,128)(2,1)S(1)}, u32[]{:S(2)}, u32[]{:S(2)}) collective-permute-start(bf16[256,2048]{1,0:T(8,128)(2,1)S(1)} %bitcast_multiply_fusion.own_ref), channel_id=1, source_target_pairs={{0,1},{1,0},{2,3},{3,2},{4,5},{5,4},{6,7},{7,6},{8,9},{9,8},{10,11... | collective-permute-start | bytes 3145736 | tf_op jit(solution)/shard_map/ppermute | solution.py:173
  27.0 27.5 %copy-start = (bf16[256,2048]{1,0:T(8,128)(2,1)S(1)}, bf16[256,2048]{1,0:T(8,128)(2,1)}, u32[]{:S(2)}) copy-start(bf16[256,2048]{1,0:T(8,128)(2,1)} %codes.1.code_ref) | copy-start | bytes 3145732

commit v8 on v7

--- a/solution.py
+++ b/solution.py
@@ -138,9 +138,9 @@
         for j in range(CAP)
     ]
     sums = [None, None]
-    for first in range(0, CT, 2):
+    for first in range(0, CT, 4):
         values = []
-        for t in (first, first + 1):
+        for t in range(first, first + 4):
             code_t = code_ref[:, t * TW : (t + 1) * TW]
             value = jnp.zeros((rows, TW), BF16)
             for d in range(DROP + 1):
@@ -149,7 +149,7 @@
             values.append(value)
         used = jnp.concatenate(values, axis=1)
         for i, ref in enumerate((own_ref, other_ref)):
-            part = ref[:, first * TW : (first + 2) * TW]
+            part = ref[:, first * TW : (first + 4) * TW]
             more = lax.dot_general(used, part, (((1,), (1,)), ((), ())), preferred_element_type=F32)
             sums[i] = more if sums[i] is None else sums[i] + more
     for total, column in ((sums[0], core), (sums[1], 1 - core)):

time: 87.1 us -> 87.1 us (level)
  no operation moved by 1% of the time
where the time goes in v8:
time: 87.1 us; the launch traced here: 86.8 us
  blocking collectives  45.5 us (52%)
  starting transfers between devices  20.3 us (23%)
  waiting for transfers between devices  12.7 us (15%)
  Pallas kernels  6.34 us (7%)
  other arithmetic  1.56 us (2%)
    all_to_all x1, starting transfers between devices, per_device(): arrived = lax.all_to_all(packed, ('z', 'y'), 0, 0, tiled=True)  18.4 us
    all_to_all x1, blocking collectives, per_device(): sums = lax.all_to_all(sums, 'z', 0, 0, tiled=True).sum(axis=0)  16.7 us
    all_gather x1, blocking collectives, per_device(): gathered = lax.all_gather(slots, 'x', axis=0, tiled=True)  14.7 us
    all_to_all x1, blocking collectives, per_device(): sums = lax.all_to_all(sums, ('x', 'y'), 0, 0, tiled=True)  14.1 us
    all_to_all x1, waiting for transfers between devices, per_device(): arrived = lax.all_to_all(packed, ('z', 'y'), 0, 0, tiled=True)  12.7 us
    pallas_call x1, Pallas kernels, codes_of(): pl.pallas_call(codes_kernel, out_shape=jax.ShapeDtypeStruct((NX * NW, CT...  3.29 us
    pallas_call x1, Pallas kernels, pack(): pl.pallas_call(pack_kernel, out_shape=jax.ShapeDtypeStruct((NW, 4, CAP //...  2.17 us
    ppermute x1, starting transfers between devices, per_device(): other = lax.ppermute(own, 'c', [(0, 1), (1, 0)])  1.92 us
  transfers between devices with their start and end apart: 2, of which 1 were waited for; matrix products, arithmetic and copies ran while one was open for 1% of the time, Pallas kernels for 4%

profile of v8, /device:TPU:32, one launch (start us, length us, event | category | flops | bytes accessed | tf_op | source)
XLA Modules:
  0.0 86.8 jit_solution(12811036996613491996)
XLA Ops:
  0.0 0.0 copy-start.2
  0.0 0.0 copy-start.1
  0.0 2.2 %pack.1 = bf16[64,4,384]{2,1,0:T(4,128)(2,1)} custom-call(s32[512,1024]{1,0:T(8,128)} %live_ref.3, bf16[1,131072]{1,0:T(2,128)(2,1)} %amp_ref.1), custom_call_target="tpu_custom_call" | custom-call | tf_op jit(solution)/shard_map/pack/pallas_call | solution.py:78
  2.2 18.4 %all-to-all-start = ((bf16[64,4,384]{2,1,0:T(4,128)(2,1)}), bf16[64,4,384]{2,1,0:T(4,128)(2,1)S(1)}, u32[]{:S(2)}, u32[]{:S(2)}) async-start(bf16[64,4,384]{2,1,0:T(4,128)(2,1)} %pack.1), calls=%async_computation | async-start | bytes 393216 | tf_op jit(solution)/shard_map/all_to_all | solution.py:175
  20.6 0.0 copy-done.2
  20.6 0.2 mul.15
  20.8 0.0 copy-done.1
  20.8 0.2 bitcast_multiply_fusion.own_ref
  21.1 1.9 %collective-permute-start = (bf16[256,2048]{1,0:T(8,128)(2,1)S(1)}, bf16[256,2048]{1,0:T(8,128)(2,1)S(1)}, u32[]{:S(2)}, u32[]{:S(2)}) collective-permute-start(bf16[256,2048]{1,0:T(8,128)(2,1)S(1)} %bitcast_multiply_fusion.own_ref), channel_id=1, source_target_pairs={{0,1},{1,0},{2,3},{3,2},{4,5},{5,4},{6,7},{7,6},{8,9},{9,8},{10,11... | collective-permute-start | bytes 3145736 | tf_op jit(solution)/shard_map/ppermute | solution.py:173
  23.0 0.7 pad_add_fusion.ids_ref
  23.7 3.3 %codes.1.code_ref = bf16[256,2048]{1,0:T(8,128)(2,1)} custom-call(s32[2]{0:T(128)} %pad_add_fusion.ids_ref, s32[512,1024]{1,0:T(8,128)} %live_ref.3), custom_call_target="tpu_custom_call" | custom-call | tf_op jit(solution)/shard_map/codes/pallas_call | solution.py:120
  27.0 0.0 copy-start
  27.0 12.7 %all-to-all-done = bf16[64,4,384]{2,1,0:T(4,128)(2,1)S(1)} async-done(((bf16[64,4,384]{2,1,0:T(4,128)(2,1)}), bf16[64,4,384]{2,1,0:T(4,128)(2,1)S(1)}, u32[]{:S(2)}, u32[]{:S(2)}) %all-to-all-start) | async-done | bytes 196640 | tf_op jit(solution)/shard_map/all_to_all | solution.py:175
  39.7 14.7 %all_gather.3.amp_ref = bf16[16,64,384]{2,1,0:T(8,128)(2,1)S(1)} all-gather(bf16[4,64,384]{2,1,0:T(8,128)(2,1)S(1)} %bitcast.19), channel_id=1, replica_groups=mesh['z'=16,'y'=4,'x'=4,'c'=2] {'x'}, dimensions={0}, use_global_device_ids=true | all-gather | bytes 983040 | tf_op jit(solution)/shard_map/all_gather | solution.py:177
  54.4 0.0 collective-permute-done.other_ref
  54.4 0.0 copy-done
  54.4 0.9 %ladder.1 = f32[16,4,16,128]{3,2,1,0:T(8,128)S(1)} custom-call(bf16[256,2048]{1,0:T(8,128)(2,1)S(1)} %copy-done, bf16[16,64,384]{2,1,0:T(8,128)(2,1)S(1)} %all_gather.3.amp_ref, bf16[256,2048]{1,0:T(8,128)(2,1)S(1)} %bitcast_multiply_fusion.own_ref, bf16[256,2048]{1,0:T(8,128)(2,1)S(1)} %collective-permute-done.other_ref), custom_call_target="tpu_custom_call" | custom-call | tf_op jit(solution)/shard_map/ladder/pallas_call | solution.py:162
  55.3 14.1 %all_to_all.15 = f32[16,4,16,128]{3,2,1,0:T(8,128)S(1)} all-to-all(f32[16,4,16,128]{3,2,1,0:T(8,128)S(1)} %ladder.1), channel_id=1, replica_groups=mesh['z'=16,'y'=4,'x'=4,'c'=2] {'x','y'}, dimensions={0} | all-to-all | bytes 1048576 | tf_op jit(solution)/shard_map/all_to_all | solution.py:180
  69.5 16.7 %all_to_all.16 = f32[16,16,128]{2,1,0:T(8,128)S(1)} all-to-all(f32[16,16,128]{2,1,0:T(8,128)S(1)} %bitcast.21), channel_id=1, replica_groups=mesh['z'=16,'y'=4,'x'=4,'c'=2] {'z'}, dimensions={0} | all-to-all | bytes 262144 | tf_op jit(solution)/shard_map/all_to_all | solution.py:183
  86.2 0.6 convert_element_type.7
  (5 shorter events, 0.1 us)
Async XLA Ops:
  0.0 20.6 %copy-start.2 = (s32[2,16]{1,0:T(2,128)S(1)}, s32[2,16]{1,0:T(2,128)}, u32[]{:S(2)}) copy-start(s32[2,16]{1,0:T(2,128)} %param.7) | copy-start | bytes 388
  0.0 20.8 %copy-start.1 = (bf16[256,2048]{1,0:T(8,128)(2,1)S(1)}, bf16[256,2048]{1,0:T(8,128)(2,1)}, u32[]{:S(2)}) copy-start(bf16[256,2048]{1,0:T(8,128)(2,1)} %param.6) | copy-start | bytes 3145732
  2.2 37.5 %all-to-all-start = ((bf16[64,4,384]{2,1,0:T(4,128)(2,1)}), bf16[64,4,384]{2,1,0:T(4,128)(2,1)S(1)}, u32[]{:S(2)}, u32[]{:S(2)}) async-start(bf16[64,4,384]{2,1,0:T(4,128)(2,1)} %pack.1), calls=%async_computation | async-start | bytes 393216 | tf_op jit(solution)/shard_map/all_to_all | solution.py:175
  21.1 33.3 %collective-permute-start = (bf16[256,2048]{1,0:T(8,128)(2,1)S(1)}, bf16[256,2048]{1,0:T(8,128)(2,1)S(1)}, u32[]{:S(2)}, u32[]{:S(2)}) collective-permute-start(bf16[256,2048]{1,0:T(8,128)(2,1)S(1)} %bitcast_multiply_fusion.own_ref), channel_id=1, source_target_pairs={{0,1},{1,0},{2,3},{3,2},{4,5},{5,4},{6,7},{7,6},{8,9},{9,8},{10,11... | collective-permute-start | bytes 3145736 | tf_op jit(solution)/shard_map/ppermute | solution.py:173
  27.0 27.5 %copy-start = (bf16[256,2048]{1,0:T(8,128)(2,1)S(1)}, bf16[256,2048]{1,0:T(8,128)(2,1)}, u32[]{:S(2)}) copy-start(bf16[256,2048]{1,0:T(8,128)(2,1)} %codes.1.code_ref) | copy-start | bytes 3145732
